TPU v7x, 256 devices: a whole 4x4x8 slice. The times are simulated.
256 devices in a mesh: dp: 4 (over x), expert: 64 (over y, z, core).
Axes of the slice: x: 4, y: 4, z: 8, core: 2. Of those that a mesh axis runs over, the one named last changes fastest.
Arguments:
- tokens: bfloat16 [8192, 2048], P('expert'), may hold values from -4 to 4
- norm_gain: bfloat16 [2048], replicated, may hold values from 0.5 to 1.5
- routing_projection_matrix: bfloat16 [2048, 64], replicated, may hold values from -0.125 to 0.125
- experts: int32 [8192, 8], P('expert'), may hold values from 0 to 63, as said below
- replica_key: int32 [8192, 8], P('expert'), may hold values from 0 to 1048575
- slot_expert: int32 [128], replicated, may hold values from 0 to 63, as said below
- capacity: int32 [128], replicated, may hold values from 4 to 16, as said below
- slot_gate_up_weight: bfloat16 [128, 2048, 2, 1024], P('expert', None, None, 'dp'), may hold values from -0.125 to 0.125
- down_weight: bfloat16 [128, 1024, 2048], P('expert', 'dp'), may hold values from -0.1875 to 0.1875
Outputs:
- mixed: bfloat16 [8192, 2048], P('expert', 'dp')
Inputs may be any that keep to these rules, and one draw needn't show every extreme that they name: Each row names 8 different experts. `slot_expert`: every expert occupies at least one slot. `capacity`: for every j the capacities of slots 2 * j and 2 * j + 1 sum to at most 24, and to exactly 24 for some j.
All inputs are finite; a program needn't handle non-finite values.
Results may differ from a plain program's by a relative error of at most 0.012.
Values may be sent and summed in bfloat16 or wider, within the bound.
A program may use at most 128 MiB of HBM per device.

v0:
```python
import jax
import jax.numpy as jnp
from jax import lax
from jax.sharding import PartitionSpec as P

CAPACITY_HIGH = 16


def assign_slots(experts, replica_key, slot_expert):
    flat_experts = experts.reshape(-1)
    holders = (flat_experts[:, None] == slot_expert[None, :]).astype(jnp.int32)
    copies = jnp.sum(holders, axis=1)
    earlier = jnp.cumsum(holders, axis=1) - holders
    wanted = replica_key.reshape(-1) % copies
    matched = holders * (earlier == wanted[:, None]).astype(jnp.int32)
    numbers = jnp.arange(slot_expert.shape[0], dtype=jnp.int32)
    return jnp.sum(matched * numbers[None, :], axis=1)


def expert_part(rows, gate_up_one, down_one):
    model_width = rows.shape[2]
    unit_count = gate_up_one.shape[2]
    flat_rows = rows.reshape(-1, model_width)
    gate_up_out = jnp.dot(
        flat_rows,
        gate_up_one.reshape(model_width, 2 * unit_count),
        preferred_element_type=jnp.float32,
    )
    activated = (jax.nn.silu(gate_up_out[:, :unit_count]) * gate_up_out[:, unit_count:]).astype(
        jnp.bfloat16
    )
    result = jnp.dot(activated, down_one, preferred_element_type=jnp.float32)
    result = lax.optimization_barrier(result.astype(jnp.bfloat16))
    return result.reshape(rows.shape)


def combine(returned, target, weight_kept, rows_here, pick_count):
    flat_rows = returned.reshape(-1, returned.shape[2])
    flat_rows = jnp.concatenate([flat_rows, jnp.zeros((1, flat_rows.shape[1]), flat_rows.dtype)])
    gathered = flat_rows[target].astype(jnp.float32).reshape(rows_here, pick_count, -1)
    return jnp.sum(weight_kept.reshape(rows_here, pick_count)[:, :, None] * gathered, axis=1)


def on_device(
    tokens,
    norm_gain,
    routing_projection_matrix,
    experts,
    replica_key,
    slot_expert,
    capacity,
    slot_gate_up_weight,
    down_weight,
):
    peer_count = lax.axis_size("expert")
    group_pos = lax.axis_index("dp")
    rows_here = tokens.shape[0]
    model_width = tokens.shape[1]
    pick_count = experts.shape[1]
    slot_count = slot_expert.shape[0]
    per_device = slot_count // peer_count
    quarter = model_width // lax.axis_size("dp")
    hidden = tokens.astype(jnp.float32)
    scale = lax.rsqrt(jnp.mean(hidden * hidden, axis=-1, keepdims=True) + 1e-06)
    normed = (hidden * scale * norm_gain.astype(jnp.float32)).astype(jnp.bfloat16)
    logits = jnp.dot(normed, routing_projection_matrix, preferred_element_type=jnp.float32)
    routing_logit_matrix = jax.nn.sigmoid(jnp.take_along_axis(logits, experts, axis=1)).reshape(-1)
    slot_ids = assign_slots(experts, replica_key, slot_expert)
    onehot = (slot_ids[:, None] == jnp.arange(slot_count, dtype=jnp.int32)[None, :]).astype(
        jnp.int32
    )
    position = jnp.sum((jnp.cumsum(onehot, axis=0) - onehot) * onehot, axis=1)
    kept_mask = position < jnp.sum(onehot * capacity[None, :], axis=1)
    slot_parity = jnp.arange(slot_count, dtype=jnp.int32) % per_device
    buffer_rows = per_device * CAPACITY_HIGH
    offsets = slot_parity * CAPACITY_HIGH
    second_start = CAPACITY_HIGH
    row_in = jnp.sum(onehot * offsets[None, :], axis=1) + position
    target = jnp.where(
        kept_mask, slot_ids // per_device * buffer_rows + row_in, peer_count * buffer_rows
    )
    source_rows = jnp.arange(rows_here * pick_count, dtype=jnp.int32) // pick_count
    outgoing = (
        jnp.zeros((peer_count * buffer_rows + 1, model_width), jnp.bfloat16)
        .at[target]
        .set(normed[source_rows])
    )
    outgoing = outgoing[:-1].reshape(peer_count, buffer_rows, model_width)
    incoming = lax.all_to_all(outgoing, "expert", split_axis=0, concat_axis=0, tiled=True)
    first_rows = incoming[:, :CAPACITY_HIGH]
    second_rows = lax.dynamic_slice_in_dim(incoming, second_start, CAPACITY_HIGH, 1)
    first_out = expert_part(first_rows, slot_gate_up_weight[0], down_weight[0])
    second_out = expert_part(second_rows, slot_gate_up_weight[1], down_weight[1])
    first_full = jnp.pad(first_out, ((0, 0), (0, buffer_rows - CAPACITY_HIGH), (0, 0)))
    clamped = jnp.minimum(second_start, buffer_rows - CAPACITY_HIGH)
    second_full = lax.dynamic_update_slice(jnp.zeros_like(first_full), second_out, (0, clamped, 0))
    row_index = jnp.arange(buffer_rows, dtype=jnp.int32)[None, :, None]
    partial_value = jnp.where(row_index < second_start, first_full, second_full)
    weight_kept = jnp.where(kept_mask, routing_logit_matrix, jnp.float32(0.0))
    returned = lax.all_to_all(partial_value, "expert", split_axis=0, concat_axis=0, tiled=True)
    mixture_full = combine(returned, target, weight_kept, rows_here, pick_count)
    mixture = lax.psum_scatter(
        mixture_full.astype(jnp.bfloat16), "dp", scatter_dimension=1, tiled=True
    ).astype(jnp.float32)
    residual = lax.dynamic_slice_in_dim(tokens, group_pos * quarter, quarter, 1).astype(jnp.float32)
    return (residual + mixture).astype(jnp.bfloat16)


def solution(mesh):
    in_specs = (
        P("expert", None),
        P(),
        P(),
        P("expert", None),
        P("expert", None),
        P(),
        P(),
        P("expert", None, None, "dp"),
        P("expert", "dp", None),
    )
    out_specs = P("expert", "dp")
    return jax.shard_map(
        on_device, mesh=mesh, in_specs=in_specs, out_specs=out_specs, check_vma=False
    )
```

profile of v0, /device:TPU:89, one launch (start us, length us, event | category | flops | bytes accessed | tf_op | source)
XLA Modules:
  0.0 518.2 jit_solution(1398483670056448341)
XLA Ops:
  6.5 0.9 copy.21
  7.5 0.8 compare_convert_fusion
  8.3 0.8 convert_reduce_fusion
  9.1 0.8 copy.22
  10.0 0.5 reduce_window_sum.26
  10.6 0.9 fusion.15
  11.5 0.2 fusion.23
  11.8 0.3 copy.24
  12.1 0.2 select_reduce_fusion
  12.6 0.2 fusion.6
  12.9 25.4 %scatter_custom_fusion = bf16[2049,2048]{1,0:T(8,128)(2,1)} fusion(s32[1024]{0:T(1024)S(1)} %bitcast.68, bf16[]{:T(256)} %constant.100.clone.1, bf16[128,2048]{1,0:T(8,128)(2,1)S(1)} %fusion.6, s32[1024]{0:T(1024)S(1)} %broadcast_clamp_fusion.1), kind=kCustom, calls=%fused_computation.7 | custom fusion | bytes 8392706 | tf_op jit(solution)/shard_map/scatter | solution.py:86
  38.2 8.3 %slice.56 = bf16[2048,2048]{1,0:T(8,128)(2,1)} slice(bf16[2049,2048]{1,0:T(8,128)(2,1)} %scatter_custom_fusion), slice={[0:2048], [0:2048]} | slice | bytes 16777216 | tf_op jit(solution)/shard_map/slice | solution.py:88
  46.5 11.7 %all-to-all-start = ((bf16[64,32,2048]{2,1,0:T(8,128)(2,1)}), bf16[64,32,2048]{2,1,0:T(8,128)(2,1)}, u32[]{:S(2)}, u32[]{:S(2)}) async-start(bf16[64,32,2048]{2,1,0:T(8,128)(2,1)} %bitcast.55), calls=%async_computation | async-start | bytes 16777216 | tf_op jit(solution)/shard_map/all_to_all | solution.py:89
  58.2 4.7 fusion.30
  62.9 1.9 copy.30
  64.8 0.5 copy.31
  65.3 175.9 %all-to-all-done = bf16[64,32,2048]{2,1,0:T(8,128)(2,1)} async-done(((bf16[64,32,2048]{2,1,0:T(8,128)(2,1)}), bf16[64,32,2048]{2,1,0:T(8,128)(2,1)}, u32[]{:S(2)}, u32[]{:S(2)}) %all-to-all-start) | async-done | bytes 8388640 | tf_op jit(solution)/shard_map/all_to_all | solution.py:89
  241.2 4.2 fusion.29
  245.4 2.3 fusion.32
  247.7 3.3 convolution_convert_fusion.1
  251.0 2.3 fusion.33
  253.3 3.3 convolution_convert_fusion
  256.6 10.3 %pad_select_fusion = bf16[64,32,2048]{2,1,0:T(8,128)(2,1)} fusion(bf16[64,16,2048]{2,1,0:T(8,128)(2,1)} %bitcast.59, bf16[64,16,2048]{2,1,0:T(8,128)(2,1)} %bitcast.58, pred[32]{0:T(512)(128)(4,1)S(1)} %iota_compare_fusion.3), kind=kLoop, calls=%fused_computation.6 | loop fusion | flops 4194304 | bytes 16777248 | tf_op jit(solution)/shard_map/jit(_where)/select_n | solution.py:98
  266.8 9.2 %all-to-all-start.1 = ((bf16[64,32,2048]{2,1,0:T(8,128)(2,1)}), bf16[64,32,2048]{2,1,0:T(8,128)(2,1)}, u32[]{:S(2)}, u32[]{:S(2)}) async-start(bf16[64,32,2048]{2,1,0:T(8,128)(2,1)} %pad_select_fusion), calls=%async_computation.1 | async-start | bytes 16777216 | tf_op jit(solution)/shard_map/all_to_all | solution.py:100
  276.5 0.3 fusion.31
  276.8 7.0 %gather_fusion.1 = f32[1024]{0:T(1024)S(1)} fusion(f32[128,64]{0,1:T(8,128)S(1)} %fusion.31, s32[1024]{0:T(1024)S(1)} %reshape.265), kind=kCustom, calls=%fused_computation.2 | custom fusion | bytes 16384 | tf_op jit(solution)/shard_map/jit(take_along_axis)/gather | solution.py:67
  284.1 174.9 %all-to-all-done.1 = bf16[64,32,2048]{2,1,0:T(8,128)(2,1)} async-done(((bf16[64,32,2048]{2,1,0:T(8,128)(2,1)}), bf16[64,32,2048]{2,1,0:T(8,128)(2,1)}, u32[]{:S(2)}, u32[]{:S(2)}) %all-to-all-start.1) | async-done | bytes 8388640 | tf_op jit(solution)/shard_map/all_to_all | solution.py:100
  459.1 8.3 %concatenate.3 = bf16[2049,2048]{1,0:T(8,128)(2,1)} pad(bf16[2048,2048]{1,0:T(8,128)(2,1)} %bitcast.15, bf16[]{:T(256)} %constant.100.clone.1), padding=0_1x0_0 | pad | bytes 16781314 | tf_op jit(solution)/shard_map/concatenate | solution.py:39
  467.3 13.3 %gather_fusion = bf16[1024,2048]{1,0:T(8,128)(2,1)} fusion(bf16[2049,2048]{1,0:T(8,128)(2,1)} %concatenate.3, s32[1024]{0:T(1024)S(1)} %broadcast_clamp_fusion), kind=kCustom, calls=%fused_computation.1 | custom fusion | bytes 8392704 | tf_op jit(solution)/shard_map/gather | solution.py:40
  480.6 7.3 %fusion = bf16[128,2048]{1,0:T(8,128)(2,1)} fusion(bf16[1024,2048]{1,0:T(8,128)(2,1)} %gather_fusion, f32[128,8]{1,0:T(8,128)S(1)} %copy.28), kind=kLoop, calls=%fused_computation.5 | loop fusion | flops 6029312 | bytes 4722688 | tf_op jit(solution)/shard_map/reduce_sum | solution.py:41
  488.0 21.5 %reduce-scatter.2.cloned.1.call-done = bf16[128,512]{1,0:T(8,128)(2,1)} async-done(((bf16[128,2048]{1,0:T(8,128)(2,1)}), bf16[128,512]{1,0:T(8,128)(2,1)}) %reduce-scatter.2.cloned.1.call-update) | async-done | bytes 131088 | tf_op jit(solution)/shard_map/reduce_scatter | solution.py:102
  509.5 1.6 add_convert_fusion
  (44 shorter events, 1.5 us)
Async XLA Ops:
  6.5 270.0 %copy-start = (bf16[2048,64]{0,1:T(8,128)(2,1)S(1)}, bf16[2048,64]{0,1:T(8,128)(2,1)}, u32[]{:S(2)}) copy-start(bf16[2048,64]{0,1:T(8,128)(2,1)} %param.11) | copy-start | bytes 786436
  6.5 5.6 %copy-start.5 = (s32[128]{0:T(128)S(1)}, s32[128]{0:T(128)}, u32[]{:S(2)}) copy-start(s32[128]{0:T(128)} %param.15) | copy-start | bytes 1540
  6.5 5.8 %copy-start.4 = (bf16[2048]{0:T(1024)(128)(2,1)S(1)}, bf16[2048]{0:T(1024)(128)(2,1)}, u32[]{:S(2)}) copy-start(bf16[2048]{0:T(1024)(128)(2,1)} %param.10) | copy-start | bytes 12292
  6.5 5.9 %copy-start.1 = (bf16[128,2048]{1,0:T(8,128)(2,1)S(1)}, bf16[128,2048]{1,0:T(8,128)(2,1)}, u32[]{:S(2)}) copy-start(bf16[128,2048]{1,0:T(8,128)(2,1)} %param.9) | copy-start | bytes 1572868
  46.5 194.7 %all-to-all-start = ((bf16[64,32,2048]{2,1,0:T(8,128)(2,1)}), bf16[64,32,2048]{2,1,0:T(8,128)(2,1)}, u32[]{:S(2)}, u32[]{:S(2)}) async-start(bf16[64,32,2048]{2,1,0:T(8,128)(2,1)} %bitcast.55), calls=%async_computation | async-start | bytes 16777216 | tf_op jit(solution)/shard_map/all_to_all | solution.py:89
  241.2 4.2 copy-start.2
  245.4 2.3 copy-start.6
  266.8 9.4 %copy-start.3 = (s32[128,8]{0,1:T(8,128)S(1)}, s32[128,8]{0,1:T(8,128)}, u32[]{:S(2)}) copy-start(s32[128,8]{0,1:T(8,128)} %param.12) | copy-start | bytes 12292
  266.8 192.2 %all-to-all-start.1 = ((bf16[64,32,2048]{2,1,0:T(8,128)(2,1)}), bf16[64,32,2048]{2,1,0:T(8,128)(2,1)}, u32[]{:S(2)}, u32[]{:S(2)}) async-start(bf16[64,32,2048]{2,1,0:T(8,128)(2,1)} %pad_select_fusion), calls=%async_computation.1 | async-start | bytes 16777216 | tf_op jit(solution)/shard_map/all_to_all | solution.py:100
  276.1 233.4 %reduce-scatter.2.cloned.1.call-start = ((), (), s32[]{:S(2)}) async-start(), calls=%async_computation.3 | async-start | bytes 655360 | tf_op jit(solution)/shard_map/reduce_scatter | solution.py:102
Sparse Core Ops, SparseCore 0:
  488.1 21.3 reduce-scatter.1
where the time goes:
time: 524 us; the launch traced here: 518 us
  waiting for transfers between devices  372 us (71%)
  local copies, waits for them, and re-layouts  76.2 us (15%)
  other arithmetic  23.2 us (4%)
  starting transfers between devices  20.9 us (4%)
  between operations  13.9 us (3%)
  matrix products  11.5 us (2%)
    all_to_all x1, waiting for transfers between devices, on_device(): lax.all_to_all(outgoing, 'expert', split_axis=0, concat_axis=0, tiled=True)  176 us
    all_to_all x1, waiting for transfers between devices, on_device(): lax.all_to_all(partial_value, 'expert', split_axis=0, concat_axis=0, tile...  175 us
    scatter x1, local copies, waits for them, and re-layouts, on_device(): outgoing = jnp.zeros((peer_count * buffer_rows + 1, model_width), jnp.bfl...  25.4 us
    reduce_scatter x1, waiting for transfers between devices, on_device(): lax.psum_scatter(mixture_full.astype(jnp.bfloat16), 'dp', scatter_dimensi...  21.5 us
    gather x1, local copies, waits for them, and re-layouts, combine(): flat_rows[target].astype(jnp.float32).reshape(rows_here, pick_count, -1)  13.3 us
    all_to_all x1, starting transfers between devices, on_device(): lax.all_to_all(outgoing, 'expert', split_axis=0, concat_axis=0, tiled=True)  11.7 us
  transfers between devices with their start and end apart: 3, of which 3 were waited for; matrix products, arithmetic and copies ran while one was open for 3% of the time, Pallas kernels for 0%

commit v1 on v0

v1 whole, which is shorter than its diff:
```python
import jax
import jax.numpy as jnp
from jax import lax
from jax.sharding import PartitionSpec as P

CAPACITY_HIGH = 16
CAP_DEV = 24


def assign_slots(experts, replica_key, slot_expert):
    flat_experts = experts.reshape(-1)
    holders = (flat_experts[:, None] == slot_expert[None, :]).astype(jnp.int32)
    copies = jnp.sum(holders, axis=1)
    earlier = jnp.cumsum(holders, axis=1) - holders
    wanted = replica_key.reshape(-1) % copies
    matched = holders * (earlier == wanted[:, None]).astype(jnp.int32)
    numbers = jnp.arange(slot_expert.shape[0], dtype=jnp.int32)
    return jnp.sum(matched * numbers[None, :], axis=1)


def slot_partial(flat_rows, gate_up_one, down_one):
    model_width = flat_rows.shape[1]
    unit_count = gate_up_one.shape[2]
    gate_up_out = jnp.dot(
        flat_rows,
        gate_up_one.reshape(model_width, 2 * unit_count),
        preferred_element_type=jnp.float32,
    )
    activated = (jax.nn.silu(gate_up_out[:, :unit_count]) * gate_up_out[:, unit_count:]).astype(
        jnp.bfloat16
    )
    result = jnp.dot(activated, down_one, preferred_element_type=jnp.float32)
    return result.astype(jnp.bfloat16)


def on_device(
    tokens,
    norm_gain,
    routing_projection_matrix,
    experts,
    replica_key,
    slot_expert,
    capacity,
    slot_gate_up_weight,
    down_weight,
):
    peer_count = lax.axis_size("expert")
    group_count = lax.axis_size("dp")
    group_pos = lax.axis_index("dp")
    me = lax.axis_index("expert")
    rows_here = tokens.shape[0]
    model_width = tokens.shape[1]
    pick_count = experts.shape[1]
    slot_count = slot_expert.shape[0]
    per_device = slot_count // peer_count
    quarter = model_width // group_count
    buffer_rows = CAP_DEV

    hidden = tokens.astype(jnp.float32)
    scale = lax.rsqrt(jnp.mean(hidden * hidden, axis=-1, keepdims=True) + 1e-06)
    normed = (hidden * scale * norm_gain.astype(jnp.float32)).astype(jnp.bfloat16)
    logits = jnp.dot(normed, routing_projection_matrix, preferred_element_type=jnp.float32)
    score = jax.nn.sigmoid(jnp.take_along_axis(logits, experts, axis=1)).reshape(-1)

    slot_ids = assign_slots(experts, replica_key, slot_expert)
    onehot = (slot_ids[:, None] == jnp.arange(slot_count, dtype=jnp.int32)[None, :]).astype(
        jnp.int32
    )
    position = jnp.sum((jnp.cumsum(onehot, axis=0) - onehot) * onehot, axis=1)
    slot_cap = jnp.sum(onehot * capacity[None, :], axis=1)
    kept_mask = position < slot_cap
    is_second = (slot_ids % per_device) == 1
    row_in = jnp.where(is_second, buffer_rows - slot_cap + position, position)
    target = jnp.where(
        kept_mask, slot_ids // per_device * buffer_rows + row_in, peer_count * buffer_rows
    )
    source_rows = jnp.arange(rows_here * pick_count, dtype=jnp.int32) // pick_count

    normed_part = lax.dynamic_slice_in_dim(normed, group_pos * quarter, quarter, 1)
    outgoing = (
        jnp.zeros((peer_count * buffer_rows + 1, quarter), jnp.bfloat16)
        .at[target]
        .set(normed_part[source_rows])
    )
    outgoing = outgoing[:-1].reshape(peer_count, buffer_rows, quarter)
    incoming_part = lax.all_to_all(outgoing, "expert", split_axis=0, concat_axis=0, tiled=True)
    incoming = lax.all_gather(incoming_part, "dp", axis=2, tiled=True)
    flat_in = incoming.reshape(peer_count * buffer_rows, model_width)

    first_out = slot_partial(flat_in, slot_gate_up_weight[0], down_weight[0])
    second_out = slot_partial(flat_in, slot_gate_up_weight[1], down_weight[1])
    first_cap = lax.dynamic_index_in_dim(capacity, me * per_device, keepdims=False)
    row_index = jnp.arange(peer_count * buffer_rows, dtype=jnp.int32) % buffer_rows
    partial_value = jnp.where((row_index < first_cap)[:, None], first_out, second_out)
    partial_value = partial_value.reshape(peer_count, buffer_rows, model_width)

    summed = lax.psum_scatter(partial_value, "dp", scatter_dimension=2, tiled=True)
    returned = lax.all_to_all(summed, "expert", split_axis=0, concat_axis=0, tiled=True)

    flat_ret = returned.reshape(peer_count * buffer_rows, quarter)
    flat_ret = jnp.concatenate([flat_ret, jnp.zeros((1, quarter), flat_ret.dtype)])
    weight_kept = jnp.where(kept_mask, score, jnp.float32(0.0))
    gathered = flat_ret[target].astype(jnp.float32).reshape(rows_here, pick_count, quarter)
    mixture = jnp.sum(weight_kept.reshape(rows_here, pick_count)[:, :, None] * gathered, axis=1)
    residual = lax.dynamic_slice_in_dim(tokens, group_pos * quarter, quarter, 1).astype(jnp.float32)
    return (residual + mixture).astype(jnp.bfloat16)


def solution(mesh):
    in_specs = (
        P("expert", None),
        P(),
        P(),
        P("expert", None),
        P("expert", None),
        P(),
        P(),
        P("expert", None, None, "dp"),
        P("expert", "dp", None),
    )
    out_specs = P("expert", "dp")
    return jax.shard_map(
        on_device, mesh=mesh, in_specs=in_specs, out_specs=out_specs, check_vma=False
    )
```

time: 524 us -> 290 us (0.55)
  waiting for transfers between devices: 372 us -> 156 us
  blocking collectives: 0 us -> 48.8 us
  local copies, waits for them, and re-layouts: 76.2 us -> 32.3 us
  other arithmetic: 23.2 us -> 7.96 us
  starting transfers between devices: 20.9 us -> 11 us
    all_to_all x2 -> x1, waiting for transfers between devices: 351 us -> 29.3 us  [on_device(): lax.all_to_all(summed, 'expert', split_axis=0, concat_axis=0, tiled=True)]
    all_gather x0 -> x1, waiting for transfers between devices: none -> 58.9 us  [on_device(): incoming = lax.all_gather(incoming_part, 'dp', axis=2, tiled=True)]
    all_to_all x0 -> x1, blocking collectives: none -> 48.8 us  [on_device(): lax.all_to_all(outgoing, 'expert', split_axis=0, concat_axis=0, tiled=True)]
    reduce_scatter x1, waiting for transfers between devices: 21.5 us -> 67.4 us  [on_device(): lax.psum_scatter(partial_value, 'dp', scatter_dimension=2, tiled=True)]
    scatter x1, local copies, waits for them, and re-layouts: 25.4 us -> 10.1 us  [on_device(): outgoing = jnp.zeros((peer_count * buffer_rows + 1, quarter), jnp.bfloat1...]
    slice x3 -> x2, local copies, waits for them, and re-layouts: 17.1 us -> 4.78 us  [the longest x1 4.68 us: on_device(): first_out = slot_partial(flat_in, slot_gate_up_weight[0], down_weight[0])]
    select_n x4 -> x3, other arithmetic: 10.4 us -> 0.09 us  [the longest x1 0.05 us: on_device(): outgoing = jnp.zeros((peer_count * buffer_rows + 1, quarter), jnp.bfloat1...]
    all_to_all x2 -> x1, starting transfers between devices: 20.9 us -> 10.8 us  [on_device(): lax.all_to_all(summed, 'expert', split_axis=0, concat_axis=0, tiled=True)]
  transfers between devices with their start and end apart: 3 -> 3, of which waited for: 3 -> 3; matrix products, arithmetic and copies ran while one was open for 3% -> 6% of each run, Pallas kernels for 0% -> 0%
where the time goes in v1:
time: 290 us; the launch traced here: 285 us
  waiting for transfers between devices  156 us (54%)
  blocking collectives  48.8 us (17%)
  local copies, waits for them, and re-layouts  32.3 us (11%)
  matrix products  15.9 us (5%)
  between operations  13.8 us (5%)
  starting transfers between devices  11 us (4%)
  other arithmetic  7.96 us (3%)
    reduce_scatter x1, waiting for transfers between devices, on_device(): lax.psum_scatter(partial_value, 'dp', scatter_dimension=2, tiled=True)  67.4 us
    all_gather x1, waiting for transfers between devices, on_device(): incoming = lax.all_gather(incoming_part, 'dp', axis=2, tiled=True)  58.9 us
    all_to_all x1, blocking collectives, on_device(): lax.all_to_all(outgoing, 'expert', split_axis=0, concat_axis=0, tiled=True)  48.8 us
    all_to_all x1, waiting for transfers between devices, on_device(): lax.all_to_all(summed, 'expert', split_axis=0, concat_axis=0, tiled=True)  29.3 us
    all_to_all x1, starting transfers between devices, on_device(): lax.all_to_all(summed, 'expert', split_axis=0, concat_axis=0, tiled=True)  10.8 us
    scatter x1, local copies, waits for them, and re-layouts, on_device(): outgoing = jnp.zeros((peer_count * buffer_rows + 1, quarter), jnp.bfloat1...  10.1 us
    dot_general x2, matrix products, slot_partial(): jnp.dot(flat_rows, gate_up_one.reshape(model_width, 2 * unit_count), pref...  9.78 us
    gather x5, local copies, waits for them, and re-layouts, on_device(): jnp.take_along_axis(logits, experts, axis=1)  7.34 us
  transfers between devices with their start and end apart: 3, of which 3 were waited for; matrix products, arithmetic and copies ran while one was open for 6% of the time, Pallas kernels for 0%

profile of v1, /device:TPU:89, one launch (start us, length us, event | category | flops | bytes accessed | tf_op | source)
XLA Modules:
  0.0 285.2 jit_solution(4413022350040989855)
XLA Ops:
  6.6 0.8 copy.21
  7.5 0.8 convert_reduce_fusion
  8.3 0.8 compare_convert_fusion
  9.0 1.2 fusion.3
  10.3 0.7 convert_element_type.50
  11.0 0.8 copy.22
  11.9 0.5 reduce_window_sum.26
  12.5 0.2 fusion.19
  12.8 0.2 fusion.23
  13.1 0.3 copy.24
  13.9 0.5 copy-done.2
  14.4 10.1 %scatter_custom_fusion = bf16[1537,512]{1,0:T(8,128)(2,1)S(1)} fusion(s32[1024]{0:T(1024)S(1)} %bitcast.69, bf16[128,512]{1,0:T(8,128)(2,1)S(1)} %constant_dynamic-slice_fusion, s32[1024]{0:T(1024)S(1)} %broadcast_clamp_fusion.1, bf16[]{:T(256)} %constant.114.clone.1), kind=kCustom, calls=%fused_computation.20 | custom fusion | bytes 1573890 | tf_op jit(solution)/shard_map/scatter | solution.py:83
  24.6 48.8 %all_to_all.10 = bf16[64,24,512]{2,1,0:T(8,128)(2,1)} all-to-all(bf16[64,24,512]{2,1,0:T(8,128)(2,1)S(1)} %bitcast.59), channel_id=1, replica_groups=mesh['dp'=4,'expert'=64] {'expert'}, dimensions={0} | all-to-all | bytes 3145728 | tf_op jit(solution)/shard_map/all_to_all | solution.py:86
  73.4 0.2 reduce-scatter.2.cloned.1.call-start
  73.7 0.6 dynamic_slice.11
  74.3 4.7 %fusion.32 = (bf16[1,2048,2,256]{3,2,1,0:T(2,128)(2,1)S(1)}, bf16[1,2048,2,256]{3,2,1,0:T(2,128)(2,1)S(1)}) fusion(bf16[2,2048,2,256]{3,2,1,0:T(2,128)(2,1)} %param.16), kind=kLoop, calls=%fused_computation.77 | loop fusion | bytes 8388608 | tf_op jit(solution)/shard_map/slice | solution.py:90
  78.9 0.5 copy.30
  79.4 1.8 copy.31
  81.3 0.7 fusion.26
  81.9 58.9 %all-gather.2.cloned.1.call-done = bf16[64,24,2048]{2,1,0:T(8,128)(2,1)} async-done(((bf16[64,24,512]{2,1,0:T(8,128)(2,1)}), bf16[64,24,2048]{2,1,0:T(8,128)(2,1)}) %all-gather.2.cloned.1.call-update) | async-done | bytes 6291472 | tf_op jit(solution)/shard_map/all_gather | solution.py:87
  140.8 6.3 %fusion.35 = f32[1536,512]{1,0:T(8,128)S(1)} fusion(bf16[1536,2048]{1,0:T(8,128)(2,1)} %bitcast.71, bf16[2048,512]{1,0:T(8,128)(2,1)} %bitcast.62), kind=kOutput, calls=%fused_computation.80 | convolution fusion | flops 3221225472 | bytes 11534336 | tf_op jit(solution)/shard_map/dot_general | solution.py:24
  147.1 3.5 %fusion.34 = f32[1536,512]{1,0:T(8,128)S(1)} fusion(bf16[1536,2048]{1,0:T(8,128)(2,1)S(1)} %bitcast.72, bf16[2048,512]{1,0:T(8,128)(2,1)S(1)} %bitcast.61), kind=kOutput, calls=%fused_computation.79 | convolution fusion | flops 3221225472 | bytes 11534336 | tf_op jit(solution)/shard_map/dot_general | solution.py:24
  150.6 1.9 convolution_convert_fusion
  152.5 3.9 %broadcast_select_fusion = bf16[1536,2048]{1,0:T(8,128)(2,1)} fusion(bf16[1536,2048]{1,0:T(8,128)(2,1)S(1)} %convolution_convert_fusion, pred[1536]{0:T(1024)(128)(4,1)S(1)} %fusion.26, bf16[2,256,2048]{2,1,0:T(8,128)(2,1)S(1)} %copy-done.8, f32[1536,512]{1,0:T(8,128)S(1)} %fusion.34), kind=kOutput, calls=%fused_computation.6 | convolution fusion | flops 1619263488 | bytes 16779264 | tf_op jit(solution)/shard_map/dot_general | solution.py:32
  156.5 67.4 %reduce-scatter.2.cloned.1.call-done = bf16[64,24,512]{2,1,0:T(8,128)(2,1)} async-done(((bf16[64,24,2048]{2,1,0:T(8,128)(2,1)}), bf16[64,24,512]{2,1,0:T(8,128)(2,1)}) %reduce-scatter.2.cloned.1.call-update) | async-done | bytes 1572880 | tf_op jit(solution)/shard_map/reduce_scatter | solution.py:97
  223.9 10.8 %all-to-all-start.1 = ((bf16[64,24,512]{2,1,0:T(8,128)(2,1)}), bf16[64,24,512]{2,1,0:T(8,128)(2,1)S(1)}, u32[]{:S(2)}, u32[]{:S(2)}) async-start(bf16[64,24,512]{2,1,0:T(8,128)(2,1)} %reduce-scatter.2.cloned.1.call-done), calls=%async_computation.2 | async-start | bytes 3145728 | tf_op jit(solution)/shard_map/all_to_all | solution.py:98
  234.9 0.3 fusion.33
  235.2 7.0 %gather_fusion.1 = f32[1024]{0:T(1024)S(1)} fusion(f32[128,64]{0,1:T(8,128)S(1)} %fusion.33, s32[1024]{0:T(1024)S(1)} %reshape.274), kind=kCustom, calls=%fused_computation.2 | custom fusion | bytes 16384 | tf_op jit(solution)/shard_map/jit(take_along_axis)/gather | solution.py:63
  242.7 29.3 %all-to-all-done.1 = bf16[64,24,512]{2,1,0:T(8,128)(2,1)S(1)} async-done(((bf16[64,24,512]{2,1,0:T(8,128)(2,1)}), bf16[64,24,512]{2,1,0:T(8,128)(2,1)S(1)}, u32[]{:S(2)}, u32[]{:S(2)}) %all-to-all-start.1) | async-done | bytes 1572896 | tf_op jit(solution)/shard_map/all_to_all | solution.py:98
  272.1 4.0 %gather_fusion = bf16[1024,512]{1,0:T(8,128)(2,1)S(1)} fusion(bf16[1537,512]{1,0:T(8,128)(2,1)S(1)} %concatenate.3, s32[1024]{0:T(1024)S(1)} %broadcast_clamp_fusion), kind=kCustom, calls=%fused_computation.1 | custom fusion | bytes 2101248 | tf_op jit(solution)/shard_map/gather | solution.py:103
  276.1 0.7 fusion
  276.8 1.6 add_convert_fusion
  (48 shorter events, 1.9 us)
Async XLA Ops:
  6.5 228.4 %copy-start = (bf16[2048,64]{0,1:T(8,128)(2,1)S(1)}, bf16[2048,64]{0,1:T(8,128)(2,1)}, u32[]{:S(2)}) copy-start(bf16[2048,64]{0,1:T(8,128)(2,1)} %param.11) | copy-start | bytes 786436
  6.5 5.9 %copy-start.5 = (s32[128]{0:T(128)S(1)}, s32[128]{0:T(128)}, u32[]{:S(2)}) copy-start(s32[128]{0:T(128)} %param.14) | copy-start | bytes 1540
  6.5 134.3 %all-gather.2.cloned.1.call-start = ((), (), s32[]{:S(2)}) async-start(), calls=%async_computation.3 | async-start | bytes 7864320 | tf_op jit(solution)/shard_map/all_gather | solution.py:87
  11.9 1.5 copy-start.1
  12.7 0.9 copy-start.6
  13.6 0.8 copy-start.2
  73.4 150.4 %reduce-scatter.2.cloned.1.call-start = ((), (), s32[]{:S(2)}) async-start(), calls=%async_computation.4 | async-start | bytes 7864320 | tf_op jit(solution)/shard_map/reduce_scatter | solution.py:97
  140.8 6.3 %copy-start.7 = (bf16[64,24,2048]{2,1,0:T(8,128)(2,1)S(1)}, bf16[64,24,2048]{2,1,0:T(8,128)(2,1)}, u32[]{:S(2)}) copy-start(bf16[64,24,2048]{2,1,0:T(8,128)(2,1)} %all-gather.2.cloned.1.call-done) | copy-start | bytes 18874372
  147.1 3.5 %copy-start.8 = (bf16[2,256,2048]{2,1,0:T(8,128)(2,1)S(1)}, bf16[2,256,2048]{2,1,0:T(8,128)(2,1)}, u32[]{:S(2)}) copy-start(bf16[2,256,2048]{2,1,0:T(8,128)(2,1)} %param.17) | copy-start | bytes 6291460
  156.4 78.2 %copy-start.4 = (s32[128,8]{0,1:T(8,128)S(1)}, s32[128,8]{0,1:T(8,128)}, u32[]{:S(2)}) copy-start(s32[128,8]{0,1:T(8,128)} %param.12) | copy-start | bytes 12292
  156.4 78.5 %copy-start.3 = (bf16[128,2048]{1,0:T(8,128)(2,1)S(1)}, bf16[128,2048]{1,0:T(8,128)(2,1)}, u32[]{:S(2)}) copy-start(bf16[128,2048]{1,0:T(8,128)(2,1)} %copy-done.2) | copy-start | bytes 1572868
  223.9 48.2 %all-to-all-start.1 = ((bf16[64,24,512]{2,1,0:T(8,128)(2,1)}), bf16[64,24,512]{2,1,0:T(8,128)(2,1)S(1)}, u32[]{:S(2)}, u32[]{:S(2)}) async-start(bf16[64,24,512]{2,1,0:T(8,128)(2,1)} %reduce-scatter.2.cloned.1.call-done), calls=%async_computation.2 | async-start | bytes 3145728 | tf_op jit(solution)/shard_map/all_to_all | solution.py:98
Sparse Core Ops, SparseCore 0:
  73.6 67.1 all-gather.1
  156.6 67.2 reduce-scatter.1

commit v2 on v1

--- a/solution.py
+++ b/solution.py
@@ -18,7 +18,7 @@
     return jnp.sum(matched * numbers[None, :], axis=1)
 
 
-def slot_partial(flat_rows, gate_up_one, down_one):
+def slot_activated(flat_rows, gate_up_one):
     model_width = flat_rows.shape[1]
     unit_count = gate_up_one.shape[2]
     gate_up_out = jnp.dot(
@@ -26,11 +26,22 @@
         gate_up_one.reshape(model_width, 2 * unit_count),
         preferred_element_type=jnp.float32,
     )
-    activated = (jax.nn.silu(gate_up_out[:, :unit_count]) * gate_up_out[:, unit_count:]).astype(
+    return (jax.nn.silu(gate_up_out[:, :unit_count]) * gate_up_out[:, unit_count:]).astype(
         jnp.bfloat16
     )
-    result = jnp.dot(activated, down_one, preferred_element_type=jnp.float32)
-    return result.astype(jnp.bfloat16)
+
+
+def group_sums(act_all, down_cols, unit_count):
+    total = None
+    for lower in range(0, act_all.shape[1], unit_count):
+        piece = jnp.dot(
+            act_all[:, lower:lower + unit_count],
+            down_cols[lower:lower + unit_count],
+            preferred_element_type=jnp.float32,
+        )
+        piece = piece.astype(jnp.bfloat16).astype(jnp.float32)
+        total = piece if total is None else total + piece
+    return total
 
 
 def on_device(
@@ -87,14 +98,19 @@
     incoming = lax.all_gather(incoming_part, "dp", axis=2, tiled=True)
     flat_in = incoming.reshape(peer_count * buffer_rows, model_width)
 
-    first_out = slot_partial(flat_in, slot_gate_up_weight[0], down_weight[0])
-    second_out = slot_partial(flat_in, slot_gate_up_weight[1], down_weight[1])
+    first_act = slot_activated(flat_in, slot_gate_up_weight[0])
+    second_act = slot_activated(flat_in, slot_gate_up_weight[1])
     first_cap = lax.dynamic_index_in_dim(capacity, me * per_device, keepdims=False)
     row_index = jnp.arange(peer_count * buffer_rows, dtype=jnp.int32) % buffer_rows
-    partial_value = jnp.where((row_index < first_cap)[:, None], first_out, second_out)
-    partial_value = partial_value.reshape(peer_count, buffer_rows, model_width)
-
-    summed = lax.psum_scatter(partial_value, "dp", scatter_dimension=2, tiled=True)
+    in_first = (row_index < first_cap)[:, None]
+    act_here = jnp.where(in_first, first_act, second_act)
+    act_all = lax.all_gather(act_here, "dp", axis=1, tiled=True)
+    down_here = lax.all_to_all(down_weight, "dp", split_axis=2, concat_axis=1, tiled=True)
+    unit_count = down_weight.shape[1]
+    first_sum = group_sums(act_all, down_here[0], unit_count)
+    second_sum = group_sums(act_all, down_here[1], unit_count)
+    expert_out = jnp.where(in_first, first_sum, second_sum).astype(jnp.bfloat16)
+    summed = expert_out.reshape(peer_count, buffer_rows, quarter)
     returned = lax.all_to_all(summed, "expert", split_axis=0, concat_axis=0, tiled=True)
 
     flat_ret = returned.reshape(peer_count * buffer_rows, quarter)

time: 290 us -> 289 us (level)
  waiting for transfers between devices: 156 us -> 109 us
  blocking collectives: 48.8 us -> 85.8 us
  local copies, waits for them, and re-layouts: 32.3 us -> 36.9 us
  matrix products: 15.9 us -> 18.9 us
    reduce_scatter x1 -> x0, waiting for transfers between devices: 67.4 us -> none  [on_device(): lax.psum_scatter(partial_value, 'dp', scatter_dimension=2, tiled=True)]
    all_to_all x0 -> x1, blocking collectives: none -> 37 us  [on_device(): lax.all_to_all(down_weight, 'dp', split_axis=2, concat_axis=1, tiled=True)]
    all_gather x0 -> x1, waiting for transfers between devices: none -> 20.4 us  [on_device(): act_all = lax.all_gather(act_here, 'dp', axis=1, tiled=True)]
    unnamed x22 -> x21, local copies, waits for them, and re-layouts: 4.48 us -> 8.87 us
    dot_general x4 -> x10, matrix products: 15.6 us -> 18.6 us  [the longest x8 9.54 us: group_sums(): jnp.dot(act_all[:, lower:lower + unit_count], down_cols[lower:lower + uni...]
  transfers between devices with their start and end apart: 3 -> 3, of which waited for: 3 -> 3; matrix products, arithmetic and copies ran while one was open for 6% -> 8% of each run, Pallas kernels for 0% -> 0%
where the time goes in v2:
time: 289 us; the launch traced here: 285 us
  waiting for transfers between devices  109 us (38%)
  blocking collectives  85.8 us (30%)
  local copies, waits for them, and re-layouts  36.9 us (13%)
  matrix products  18.9 us (7%)
  between operations  13.8 us (5%)
  starting transfers between devices  11.8 us (4%)
  other arithmetic  9.01 us (3%)
    all_gather x1, waiting for transfers between devices, on_device(): incoming = lax.all_gather(incoming_part, 'dp', axis=2, tiled=True)  58.8 us
    all_to_all x1, blocking collectives, on_device(): lax.all_to_all(outgoing, 'expert', split_axis=0, concat_axis=0, tiled=True)  48.8 us
    all_to_all x1, blocking collectives, on_device(): lax.all_to_all(down_weight, 'dp', split_axis=2, concat_axis=1, tiled=True)  37 us
    all_to_all x1, waiting for transfers between devices, on_device(): lax.all_to_all(summed, 'expert', split_axis=0, concat_axis=0, tiled=True)  29.3 us
    all_gather x1, waiting for transfers between devices, on_device(): act_all = lax.all_gather(act_here, 'dp', axis=1, tiled=True)  20.4 us
    all_to_all x1, starting transfers between devices, on_device(): lax.all_to_all(summed, 'expert', split_axis=0, concat_axis=0, tiled=True)  11.6 us
    scatter x1, local copies, waits for them, and re-layouts, on_device(): outgoing = jnp.zeros((peer_count * buffer_rows + 1, quarter), jnp.bfloat1...  10.1 us
    dot_general x8, matrix products, group_sums(): jnp.dot(act_all[:, lower:lower + unit_count], down_cols[lower:lower + uni...  9.54 us
  transfers between devices with their start and end apart: 3, of which 3 were waited for; matrix products, arithmetic and copies ran while one was open for 8% of the time, Pallas kernels for 0%

profile of v2, /device:TPU:89, one launch (start us, length us, event | category | flops | bytes accessed | tf_op | source)
XLA Modules:
  0.0 284.8 jit_solution(9664185811416828621)
XLA Ops:
  6.5 0.8 copy.58
  7.5 0.8 compare_convert_fusion
  8.2 0.8 convert_reduce_fusion
  9.0 0.8 copy.59
  10.6 0.9 fusion.20
  12.8 10.1 %scatter_custom_fusion = bf16[1537,512]{1,0:T(8,128)(2,1)S(1)} fusion(s32[1024]{0:T(1024)S(1)} %bitcast.105, bf16[128,512]{1,0:T(8,128)(2,1)S(1)} %constant_dynamic-slice_fusion, s32[1024]{0:T(1024)S(1)} %broadcast_clamp_fusion.1, bf16[]{:T(256)} %constant.114.clone.1), kind=kCustom, calls=%fused_computation.24 | custom fusion | bytes 1573890 | tf_op jit(solution)/shard_map/scatter | solution.py:94
  23.1 48.8 %all_to_all.25 = bf16[64,24,512]{2,1,0:T(8,128)(2,1)} all-to-all(bf16[64,24,512]{2,1,0:T(8,128)(2,1)S(1)} %bitcast.94), channel_id=1, replica_groups=mesh['dp'=4,'expert'=64] {'expert'}, dimensions={0} | all-to-all | bytes 3145728 | tf_op jit(solution)/shard_map/all_to_all | solution.py:97
  72.1 4.7 %fusion.31 = (bf16[1,2048,2,256]{3,2,1,0:T(2,128)(2,1)S(1)}, bf16[1,2048,2,256]{3,2,1,0:T(2,128)(2,1)S(1)}) fusion(bf16[2,2048,2,256]{3,2,1,0:T(2,128)(2,1)} %param.16), kind=kLoop, calls=%fused_computation.92 | loop fusion | bytes 8388608 | tf_op jit(solution)/shard_map/slice | solution.py:102
  77.3 1.9 copy.78
  79.2 0.6 dynamic_slice.11
  79.8 0.7 fusion.27
  80.4 58.8 %all-gather.3.cloned.1.call-done = bf16[64,24,2048]{2,1,0:T(8,128)(2,1)} async-done(((bf16[64,24,512]{2,1,0:T(8,128)(2,1)}), bf16[64,24,2048]{2,1,0:T(8,128)(2,1)}) %all-gather.3.cloned.1.call-update) | async-done | bytes 6291472 | tf_op jit(solution)/shard_map/all_gather | solution.py:98
  139.2 5.6 %fusion.33 = f32[1536,512]{1,0:T(8,128)S(1)} fusion(bf16[1536,2048]{1,0:T(8,128)(2,1)} %bitcast.107, bf16[2048,512]{1,0:T(8,128)(2,1)S(1)} %bitcast.97), kind=kOutput, calls=%fused_computation.94 | convolution fusion | flops 3221225472 | bytes 11534336 | tf_op jit(solution)/shard_map/dot_general | solution.py:24
  144.9 3.4 %fusion.34 = f32[1536,512]{1,0:T(8,128)S(1)} fusion(bf16[1536,2048]{1,0:T(8,128)(2,1)S(1)} %bitcast.108, bf16[2048,512]{1,0:T(8,128)(2,1)S(1)} %bitcast.98), kind=kOutput, calls=%fused_computation.95 | convolution fusion | flops 3221225472 | bytes 11534336 | tf_op jit(solution)/shard_map/dot_general | solution.py:24
  148.3 2.1 fusion.9
  150.5 4.8 %copy.66 = bf16[2,256,2048]{1,0,2:T(2,128)(2,1)S(1)} copy(bf16[2,256,2048]{2,1,0:T(8,128)(2,1)} %param.17) | data formatting | bytes 4194304 | tf_op args[8]
  155.3 37.0 %all_to_all.26 = bf16[2,256,2048]{1,0,2:T(2,128)(2,1)S(1)} all-to-all(bf16[2,256,2048]{1,0,2:T(2,128)(2,1)S(1)} %copy.66), channel_id=1, replica_groups=mesh['dp'=4,'expert'=64] {'dp'}, dimensions={2} | all-to-all | bytes 4194304 | tf_op jit(solution)/shard_map/all_to_all | solution.py:108
  192.6 20.4 %all-gather.5.cloned.1.call-done = bf16[1536,1024]{1,0:T(8,128)(2,1)} async-done(((bf16[1536,256]{1,0:T(8,128)(2,1)}), bf16[1536,1024]{1,0:T(8,128)(2,1)}) %all-gather.5.cloned.1.call-update) | async-done | bytes 3145744 | tf_op jit(solution)/shard_map/all_gather | solution.py:107
  213.0 1.9 convolution_convert_fusion
  214.9 1.7 convolution_convert_fusion.1
  216.7 0.6 convolution_convert_fusion.2
  217.3 0.6 convolution_convert_fusion.3
  217.9 0.6 convolution_convert_fusion.4
  218.5 0.6 convolution_convert_fusion.5
  219.1 0.6 convolution_convert_fusion.6
  219.8 2.9 %select_convert_fusion = bf16[1536,512]{1,0:T(8,128)(2,1)} fusion(bf16[1536,512]{1,0:T(8,128)(2,1)S(1)} %convolution_convert_fusion, bf16[1536,512]{1,0:T(8,128)(2,1)S(1)} %convolution_convert_fusion.1, bf16[1536,512]{1,0:T(8,128)(2,1)S(1)} %convolution_convert_fusion.2, bf16[1536,512]{1,0:T(8,128)(2,1)S(1)} %convolution_convert_fusion.3, ...), kind=kOutput, calls=%fused_computation.4 | convolution fusion | flops 416022528 | bytes 13633536 | tf_op jit(solution)/shard_map/dot_general | solution.py:37
  222.6 11.6 %all-to-all-start.2 = ((bf16[64,24,512]{2,1,0:T(8,128)(2,1)}), bf16[64,24,512]{2,1,0:T(8,128)(2,1)S(1)}, u32[]{:S(2)}, u32[]{:S(2)}) async-start(bf16[64,24,512]{2,1,0:T(8,128)(2,1)} %bitcast.96), calls=%async_computation.2 | async-start | bytes 3145728 | tf_op jit(solution)/shard_map/all_to_all | solution.py:114
  235.0 7.0 %gather_fusion.1 = f32[1024]{0:T(1024)S(1)} fusion(f32[128,64]{0,1:T(8,128)S(1)} %fusion.32, s32[1024]{0:T(1024)S(1)} %reshape.286), kind=kCustom, calls=%fused_computation.2 | custom fusion | bytes 16384 | tf_op jit(solution)/shard_map/jit(take_along_axis)/gather | solution.py:74
  242.3 29.3 %all-to-all-done.2 = bf16[64,24,512]{2,1,0:T(8,128)(2,1)S(1)} async-done(((bf16[64,24,512]{2,1,0:T(8,128)(2,1)}), bf16[64,24,512]{2,1,0:T(8,128)(2,1)S(1)}, u32[]{:S(2)}, u32[]{:S(2)}) %all-to-all-start.2) | async-done | bytes 1572896 | tf_op jit(solution)/shard_map/all_to_all | solution.py:114
  271.7 4.0 %gather_fusion = bf16[1024,512]{1,0:T(8,128)(2,1)S(1)} fusion(bf16[1537,512]{1,0:T(8,128)(2,1)S(1)} %concatenate.3, s32[1024]{0:T(1024)S(1)} %broadcast_clamp_fusion), kind=kCustom, calls=%fused_computation.1 | custom fusion | bytes 2101248 | tf_op jit(solution)/shard_map/gather | solution.py:119
  275.7 0.7 fusion
  276.4 1.6 add_convert_fusion
  (56 shorter events, 4.3 us)
Async XLA Ops:
  6.5 228.1 %copy-start = (bf16[2048,64]{0,1:T(8,128)(2,1)S(1)}, bf16[2048,64]{0,1:T(8,128)(2,1)}, u32[]{:S(2)}) copy-start(bf16[2048,64]{0,1:T(8,128)(2,1)} %param.11) | copy-start | bytes 786436
  6.5 132.7 %all-gather.3.cloned.1.call-start = ((), (), s32[]{:S(2)}) async-start(), calls=%async_computation.3 | async-start | bytes 7864320 | tf_op jit(solution)/shard_map/all_gather | solution.py:98
  9.9 2.2 copy-start.5
  9.9 2.2 copy-start.2
  10.4 1.9 copy-start.6
  71.9 141.2 %all-gather.5.cloned.1.call-start = ((), (), s32[]{:S(2)}) async-start(), calls=%async_computation.4 | async-start | bytes 3932160 | tf_op jit(solution)/shard_map/all_gather | solution.py:107
  139.2 5.6 %copy-start.3 = (bf16[256,8,2,256]{3,1,2,0:T(8,128)(2,1)S(1)}, bf16[256,8,2,256]{3,1,2,0:T(8,128)(2,1)}, u32[]{:S(2)}) copy-start(bf16[256,8,2,256]{3,1,2,0:T(8,128)(2,1)} %copy.78) | copy-start | bytes 6291460
  139.2 5.7 %copy-start.7 = (bf16[64,24,2048]{2,1,0:T(8,128)(2,1)S(1)}, bf16[64,24,2048]{2,1,0:T(8,128)(2,1)}, u32[]{:S(2)}) copy-start(bf16[64,24,2048]{2,1,0:T(8,128)(2,1)} %all-gather.3.cloned.1.call-done) | copy-start | bytes 18874372
  213.0 3.6 %copy-start.1 = (bf16[1536,1024]{1,0:T(8,128)(2,1)S(1)}, bf16[1536,1024]{1,0:T(8,128)(2,1)}, u32[]{:S(2)}) copy-start(bf16[1536,1024]{1,0:T(8,128)(2,1)} %all-gather.5.cloned.1.call-done) | copy-start | bytes 9437188
  222.6 11.8 %copy-start.4 = (s32[128,8]{0,1:T(8,128)S(1)}, s32[128,8]{0,1:T(8,128)}, u32[]{:S(2)}) copy-start(s32[128,8]{0,1:T(8,128)} %param.12) | copy-start | bytes 12292
  222.6 48.9 %all-to-all-start.2 = ((bf16[64,24,512]{2,1,0:T(8,128)(2,1)}), bf16[64,24,512]{2,1,0:T(8,128)(2,1)S(1)}, u32[]{:S(2)}, u32[]{:S(2)}) async-start(bf16[64,24,512]{2,1,0:T(8,128)(2,1)} %bitcast.96), calls=%async_computation.2 | async-start | bytes 3145728 | tf_op jit(solution)/shard_map/all_to_all | solution.py:114
Sparse Core Ops, SparseCore 0:
  72.0 67.1 all-gather.2
  150.6 62.4 all-gather.4

commit v3 on v2

--- a/solution.py
+++ b/solution.py
@@ -1,10 +1,123 @@
+import functools
+
 import jax
 import jax.numpy as jnp
 from jax import lax
+from jax.experimental import pallas as pl
+from jax.experimental.pallas import tpu as pltpu
 from jax.sharding import PartitionSpec as P
+
+MESH = pl.DeviceIdType.MESH
 
 CAPACITY_HIGH = 16
 CAP_DEV = 24
+
+
+def exchange_kernel(n_exp, n_dp, with_down, *refs):
+    if with_down:
+        send_ref, down_ref, recv_ref, down_out, a_send, a_recv, d_send, d_recv, local_sem = refs
+    else:
+        send_ref, recv_ref, a_send, a_recv, local_sem = refs
+    me = lax.axis_index("expert")
+    gi = lax.axis_index("dp")
+
+    def a2a_copy(j, recv_slot):
+        return pltpu.make_async_remote_copy(
+            src_ref=send_ref.at[j],
+            dst_ref=recv_ref.at[recv_slot],
+            send_sem=a_send.at[j],
+            recv_sem=a_recv.at[recv_slot],
+            device_id=(gi, j),
+            device_id_type=MESH,
+        )
+
+    def down_copy(g, recv_slot):
+        q = down_out.shape[-1]
+        cols = pl.ds(pl.multiple_of(g * q, 128), q)
+        return pltpu.make_async_remote_copy(
+            src_ref=down_ref.at[:, :, cols],
+            dst_ref=down_out.at[recv_slot],
+            send_sem=d_send.at[g],
+            recv_sem=d_recv.at[recv_slot],
+            device_id=(g, me),
+            device_id_type=MESH,
+        )
+
+    barrier = pltpu.get_barrier_semaphore()
+
+    def greet(k, carry):
+        j = lax.rem(me + k, n_exp)
+        pl.semaphore_signal(barrier, 1, device_id=(gi, j), device_id_type=MESH)
+        return carry
+
+    lax.fori_loop(1, n_exp, greet, 0)
+    greet_count = n_exp - 1
+    if with_down:
+        for k in range(1, n_dp):
+            g = lax.rem(gi + k, n_dp)
+            pl.semaphore_signal(barrier, 1, device_id=(g, me), device_id_type=MESH)
+        greet_count += n_dp - 1
+    pl.semaphore_wait(barrier, greet_count)
+
+    def send_one(k, carry):
+        j = lax.rem(me + k, n_exp)
+        a2a_copy(j, me).start()
+        return carry
+
+    lax.fori_loop(1, n_exp, send_one, 0)
+    local = pltpu.make_async_copy(send_ref.at[me], recv_ref.at[me], local_sem.at[0])
+    local.start()
+    if with_down:
+        q = down_out.shape[-1]
+        for k in range(1, n_dp):
+            down_copy(lax.rem(gi + k, n_dp), gi).start()
+        own_cols = pl.ds(pl.multiple_of(gi * q, 128), q)
+        local_down = pltpu.make_async_copy(
+            down_ref.at[:, :, own_cols], down_out.at[gi], local_sem.at[1]
+        )
+        local_down.start()
+
+    def wait_one(k, carry):
+        j = lax.rem(me + k, n_exp)
+        a2a_copy(j, me).wait_send()
+        a2a_copy(j, j).wait_recv()
+        return carry
+
+    lax.fori_loop(1, n_exp, wait_one, 0)
+    local.wait()
+    if with_down:
+        for k in range(1, n_dp):
+            g = lax.rem(gi + k, n_dp)
+            down_copy(g, gi).wait_send()
+            down_copy(g, g).wait_recv()
+        local_down.wait()
+
+
+def exchange(send, down=None, collective_id=0):
+    n_exp = lax.axis_size("expert")
+    n_dp = lax.axis_size("dp")
+    with_down = down is not None
+    any_spec = pl.BlockSpec(memory_space=pl.ANY)
+    out_shape = [jax.ShapeDtypeStruct(send.shape, send.dtype)]
+    scratch = [pltpu.SemaphoreType.DMA((n_exp,)), pltpu.SemaphoreType.DMA((n_exp,))]
+    operands = [send]
+    moved = send.size * send.dtype.itemsize
+    if with_down:
+        q = down.shape[-1] // n_dp
+        out_shape.append(jax.ShapeDtypeStruct((n_dp,) + down.shape[:-1] + (q,), down.dtype))
+        scratch += [pltpu.SemaphoreType.DMA((n_dp,)), pltpu.SemaphoreType.DMA((n_dp,))]
+        operands.append(down)
+        moved += down.size * down.dtype.itemsize
+    scratch.append(pltpu.SemaphoreType.DMA((2,)))
+    return pl.pallas_call(
+        functools.partial(exchange_kernel, n_exp, n_dp, with_down),
+        out_shape=tuple(out_shape),
+        in_specs=[any_spec] * len(operands),
+        out_specs=tuple([any_spec] * len(out_shape)),
+        scratch_shapes=scratch,
+        compiler_params=pltpu.CompilerParams(collective_id=collective_id, has_side_effects=True),
+        cost_estimate=pl.CostEstimate(flops=0, transcendentals=0, bytes_accessed=2 * moved),
+    )(*operands)
 
 
 def assign_slots(experts, replica_key, slot_expert):
@@ -94,7 +207,7 @@
         .set(normed_part[source_rows])
     )
     outgoing = outgoing[:-1].reshape(peer_count, buffer_rows, quarter)
-    incoming_part = lax.all_to_all(outgoing, "expert", split_axis=0, concat_axis=0, tiled=True)
+    incoming_part, down_parts = exchange(outgoing, down_weight, collective_id=0)
     incoming = lax.all_gather(incoming_part, "dp", axis=2, tiled=True)
     flat_in = incoming.reshape(peer_count * buffer_rows, model_width)
 
@@ -105,13 +218,13 @@
     in_first = (row_index < first_cap)[:, None]
     act_here = jnp.where(in_first, first_act, second_act)
     act_all = lax.all_gather(act_here, "dp", axis=1, tiled=True)
-    down_here = lax.all_to_all(down_weight, "dp", split_axis=2, concat_axis=1, tiled=True)
+    down_here = jnp.swapaxes(down_parts, 0, 1).reshape(per_device, -1, quarter)
     unit_count = down_weight.shape[1]
     first_sum = group_sums(act_all, down_here[0], unit_count)
     second_sum = group_sums(act_all, down_here[1], unit_count)
     expert_out = jnp.where(in_first, first_sum, second_sum).astype(jnp.bfloat16)
     summed = expert_out.reshape(peer_count, buffer_rows, quarter)
-    returned = lax.all_to_all(summed, "expert", split_axis=0, concat_axis=0, tiled=True)
+    (returned,) = exchange(summed, collective_id=1)
 
     flat_ret = returned.reshape(peer_count * buffer_rows, quarter)
     flat_ret = jnp.concatenate([flat_ret, jnp.zeros((1, quarter), flat_ret.dtype)])

time: 289 us -> 270 us (0.934)
  Pallas kernels: 0 us -> 90.4 us
  blocking collectives: 85.8 us -> 0 us
  starting transfers between devices: 11.8 us -> 0.22 us
  waiting for transfers between devices: 109 us -> 99.4 us
    pallas_call x0 -> x2, Pallas kernels: none -> 90.4 us  [exchange(): pl.pallas_call(functools.partial(exchange_kernel, n_exp, n_dp, with_down)...]
    all_to_all x2 -> x0, blocking collectives: 85.8 us -> none  [the longest x1 48.8 us: on_device(): lax.all_to_all(outgoing, 'expert', split_axis=0, concat_axis=0, tiled=True)]
    all_to_all x1 -> x0, waiting for transfers between devices: 29.3 us -> none  [on_device(): lax.all_to_all(summed, 'expert', split_axis=0, concat_axis=0, tiled=True)]
    all_gather x1, waiting for transfers between devices: 20.4 us -> 37.7 us  [on_device(): act_all = lax.all_gather(act_here, 'dp', axis=1, tiled=True)]
    all_to_all x1 -> x0, starting transfers between devices: 11.6 us -> none  [on_device(): lax.all_to_all(summed, 'expert', split_axis=0, concat_axis=0, tiled=True)]
    unnamed x21 -> x22, local copies, waits for them, and re-layouts: 8.87 us -> 4.1 us
  transfers between devices with their start and end apart: 3 -> 2, of which waited for: 3 -> 2; matrix products, arithmetic and copies ran while one was open for 8% -> 6% of each run, Pallas kernels for 0% -> 0%
where the time goes in v3:
time: 270 us; the launch traced here: 266 us
  waiting for transfers between devices  99.4 us (37%)
  Pallas kernels  90.4 us (33%)
  local copies, waits for them, and re-layouts  34.5 us (13%)
  matrix products  18.6 us (7%)
  between operations  13.8 us (5%)
  other arithmetic  9.19 us (3%)
    pallas_call x2, Pallas kernels, exchange(): pl.pallas_call(functools.partial(exchange_kernel, n_exp, n_dp, with_down)...  90.4 us
    all_gather x1, waiting for transfers between devices, on_device(): incoming = lax.all_gather(incoming_part, 'dp', axis=2, tiled=True)  61.6 us
    all_gather x1, waiting for transfers between devices, on_device(): act_all = lax.all_gather(act_here, 'dp', axis=1, tiled=True)  37.7 us
    scatter x1, local copies, waits for them, and re-layouts, on_device(): outgoing = jnp.zeros((peer_count * buffer_rows + 1, quarter), jnp.bfloat1...  10.1 us
    dot_general x8, matrix products, group_sums(): jnp.dot(act_all[:, lower:lower + unit_count], down_cols[lower:lower + uni...  9.21 us
    dot_general x2, matrix products, slot_activated(): jnp.dot(flat_rows, gate_up_one.reshape(model_width, 2 * unit_count), pref...  9.05 us
    gather x5, local copies, waits for them, and re-layouts, on_device(): jnp.take_along_axis(logits, experts, axis=1)  7.34 us
  transfers between devices with their start and end apart: 2, of which 2 were waited for; matrix products, arithmetic and copies ran while one was open for 6% of the time, Pallas kernels for 0%

profile of v3, /device:TPU:89, one launch (start us, length us, event | category | flops | bytes accessed | tf_op | source)
XLA Modules:
  0.0 266.0 jit_solution(3617735431927308458)
XLA Ops:
  6.6 0.8 copy.21
  7.5 0.8 convert_reduce_fusion
  8.3 0.8 compare_convert_fusion
  9.0 1.2 fusion.3
  10.3 0.7 convert_element_type.95
  11.0 0.8 copy.22
  13.9 10.1 %scatter_custom_fusion = bf16[1537,512]{1,0:T(8,128)(2,1)S(1)} fusion(s32[1024]{0:T(1024)S(1)} %bitcast.96, bf16[128,512]{1,0:T(8,128)(2,1)S(1)} %constant_dynamic-slice_fusion, s32[1024]{0:T(1024)S(1)} %broadcast_clamp_fusion.1, bf16[]{:T(256)} %constant.114.clone.1), kind=kCustom, calls=%fused_computation.24 | custom fusion | bytes 1573890 | tf_op jit(solution)/shard_map/scatter | solution.py:207
  24.0 1.3 slice.140
  25.4 45.4 %shard_map.91 = (bf16[64,24,512]{2,1,0:T(8,128)(2,1)}, bf16[4,2,256,512]{3,2,1,0:T(8,128)(2,1)}) custom-call(bf16[64,24,512]{2,1,0:T(8,128)(2,1)} %bitcast.77, bf16[2,256,2048]{2,1,0:T(8,128)(2,1)} %refs_1_.1), custom_call_target="tpu_custom_call" | custom-call | bytes 7340032 | tf_op jit(solution)/shard_map/pallas_call | solution.py:112
  71.1 0.6 dynamic_slice.11
  71.7 4.7 %fusion.31 = (bf16[1,2048,2,256]{3,2,1,0:T(2,128)(2,1)S(1)}, bf16[1,2048,2,256]{3,2,1,0:T(2,128)(2,1)S(1)}) fusion(bf16[2,2048,2,256]{3,2,1,0:T(2,128)(2,1)} %param.16), kind=kLoop, calls=%fused_computation.92 | loop fusion | bytes 8388608 | tf_op jit(solution)/shard_map/slice | solution.py:215
  76.3 1.9 copy.31
  78.8 0.7 fusion.27
  79.4 61.6 %all-gather.3.cloned.1.call-done = bf16[64,24,2048]{2,1,0:T(8,128)(2,1)} async-done(((bf16[64,24,512]{2,1,0:T(8,128)(2,1)}), bf16[64,24,2048]{2,1,0:T(8,128)(2,1)}) %all-gather.3.cloned.1.call-update) | async-done | bytes 6291472 | tf_op jit(solution)/shard_map/all_gather | solution.py:211
  141.1 5.6 %fusion.33 = f32[1536,512]{1,0:T(8,128)S(1)} fusion(bf16[1536,2048]{1,0:T(8,128)(2,1)} %bitcast.98, bf16[2048,512]{1,0:T(8,128)(2,1)S(1)} %bitcast.89), kind=kOutput, calls=%fused_computation.94 | convolution fusion | flops 3221225472 | bytes 11534336 | tf_op jit(solution)/shard_map/dot_general | solution.py:137
  146.7 3.4 %fusion.34 = f32[1536,512]{1,0:T(8,128)S(1)} fusion(bf16[1536,2048]{1,0:T(8,128)(2,1)S(1)} %bitcast.99, bf16[2048,512]{1,0:T(8,128)(2,1)S(1)} %bitcast.88), kind=kOutput, calls=%fused_computation.95 | convolution fusion | flops 3221225472 | bytes 11534336 | tf_op jit(solution)/shard_map/dot_general | solution.py:137
  150.2 2.1 fusion.9
  152.8 7.0 %gather_fusion.1 = f32[1024]{0:T(1024)S(1)} fusion(f32[128,64]{0,1:T(8,128)S(1)} %fusion.32, s32[1024]{0:T(1024)S(1)} %reshape.287), kind=kCustom, calls=%fused_computation.2 | custom fusion | bytes 16384 | tf_op jit(solution)/shard_map/jit(take_along_axis)/gather | solution.py:187
  160.4 37.7 %all-gather.5.cloned.1.call-done = bf16[1536,1024]{1,0:T(8,128)(2,1)} async-done(((bf16[1536,256]{1,0:T(8,128)(2,1)}), bf16[1536,1024]{1,0:T(8,128)(2,1)}) %all-gather.5.cloned.1.call-update) | async-done | bytes 3145744 | tf_op jit(solution)/shard_map/all_gather | solution.py:220
  198.1 1.9 convolution_convert_fusion.3
  199.9 1.7 convolution_convert_fusion.2
  201.6 0.6 convolution_convert_fusion.1
  202.2 0.6 convolution_convert_fusion
  202.8 0.6 convolution_convert_fusion.4
  203.4 0.6 convolution_convert_fusion.5
  203.9 0.6 convolution_convert_fusion.6
  204.5 2.8 %select_convert_fusion = bf16[1536,512]{1,0:T(8,128)(2,1)} fusion(bf16[1536,512]{1,0:T(8,128)(2,1)S(1)} %convolution_convert_fusion, bf16[1536,512]{1,0:T(8,128)(2,1)S(1)} %convolution_convert_fusion.1, bf16[1536,512]{1,0:T(8,128)(2,1)S(1)} %convolution_convert_fusion.2, bf16[1536,512]{1,0:T(8,128)(2,1)S(1)} %convolution_convert_fusion.3, ...), kind=kOutput, calls=%fused_computation.4 | convolution fusion | flops 416022528 | bytes 13633536 | tf_op jit(solution)/shard_map/dot_general | solution.py:150
  207.3 44.9 %shard_map.92 = bf16[64,24,512]{2,1,0:T(8,128)(2,1)} custom-call(bf16[64,24,512]{2,1,0:T(8,128)(2,1)} %bitcast.79), custom_call_target="tpu_custom_call" | custom-call | bytes 3145728 | tf_op jit(solution)/shard_map/pallas_call | solution.py:112
  252.3 1.5 concatenate.3
  253.8 4.0 %gather_fusion = bf16[1024,512]{1,0:T(8,128)(2,1)S(1)} fusion(bf16[1537,512]{1,0:T(8,128)(2,1)S(1)} %concatenate.3, s32[1024]{0:T(1024)S(1)} %broadcast_clamp_fusion), kind=kCustom, calls=%fused_computation.1 | custom fusion | bytes 2101248 | tf_op jit(solution)/shard_map/gather | solution.py:232
  257.7 0.7 fusion
  258.4 0.7 add_convert_fusion
  (54 shorter events, 3.9 us)
Async XLA Ops:
  6.5 146.0 %copy-start = (bf16[2048,64]{0,1:T(8,128)(2,1)S(1)}, bf16[2048,64]{0,1:T(8,128)(2,1)}, u32[]{:S(2)}) copy-start(bf16[2048,64]{0,1:T(8,128)(2,1)} %param.11) | copy-start | bytes 786436
  6.5 5.9 %copy-start.6 = (s32[128]{0:T(128)S(1)}, s32[128]{0:T(128)}, u32[]{:S(2)}) copy-start(s32[128]{0:T(128)} %param.14) | copy-start | bytes 1540
  6.5 134.5 %all-gather.3.cloned.1.call-start = ((), (), s32[]{:S(2)}) async-start(), calls=%async_computation | async-start | bytes 7864320 | tf_op jit(solution)/shard_map/all_gather | solution.py:211
  11.9 1.5 copy-start.2
  12.7 0.9 copy-start.7
  70.8 127.2 %all-gather.5.cloned.1.call-start = ((), (), s32[]{:S(2)}) async-start(), calls=%async_computation.1 | async-start | bytes 3932160 | tf_op jit(solution)/shard_map/all_gather | solution.py:220
  141.1 5.6 %copy-start.4 = (bf16[256,8,2,256]{3,1,2,0:T(8,128)(2,1)S(1)}, bf16[256,8,2,256]{3,1,2,0:T(8,128)(2,1)}, u32[]{:S(2)}) copy-start(bf16[256,8,2,256]{3,1,2,0:T(8,128)(2,1)} %copy.31) | copy-start | bytes 6291460
  141.1 5.6 %copy-start.8 = (bf16[64,24,2048]{2,1,0:T(8,128)(2,1)S(1)}, bf16[64,24,2048]{2,1,0:T(8,128)(2,1)}, u32[]{:S(2)}) copy-start(bf16[64,24,2048]{2,1,0:T(8,128)(2,1)} %all-gather.3.cloned.1.call-done) | copy-start | bytes 18874372
  150.2 2.1 copy-start.5
  152.8 45.2 %copy-start.3 = (bf16[4,2,256,512]{3,2,1,0:T(8,128)(2,1)S(1)}, bf16[4,2,256,512]{3,2,1,0:T(8,128)(2,1)}, u32[]{:S(2)}) copy-start(bf16[4,2,256,512]{3,2,1,0:T(8,128)(2,1)} %get-tuple-element.8) | copy-start | bytes 6291460
  198.1 3.6 %copy-start.1 = (bf16[1536,1024]{1,0:T(8,128)(2,1)S(1)}, bf16[1536,1024]{1,0:T(8,128)(2,1)}, u32[]{:S(2)}) copy-start(bf16[1536,1024]{1,0:T(8,128)(2,1)} %all-gather.5.cloned.1.call-done) | copy-start | bytes 9437188
Sparse Core Ops, SparseCore 0:
  71.0 70.0 all-gather.2
  152.4 45.5 all-gather.4

commit v4 on v3

--- a/solution.py
+++ b/solution.py
@@ -120,6 +120,134 @@
     )(*operands)
 
 
+def dispatch_kernel(n_exp, n_dp, send_ref, down_ref, full_ref, down_out,
+                    a_send, a_recv, d_send, d_recv, f_send, f_recv, local_sem):
+    me = lax.axis_index("expert")
+    gi = lax.axis_index("dp")
+    q = down_out.shape[-1]
+
+    def a2a_copy(j, recv_slot):
+        return pltpu.make_async_remote_copy(
+            src_ref=send_ref.at[j],
+            dst_ref=full_ref.at[gi, recv_slot],
+            send_sem=a_send.at[j],
+            recv_sem=a_recv.at[recv_slot],
+            device_id=(gi, j),
+            device_id_type=MESH,
+        )
+
+    def down_copy(g, recv_slot):
+        cols = pl.ds(pl.multiple_of(g * q, 128), q)
+        return pltpu.make_async_remote_copy(
+            src_ref=down_ref.at[:, :, cols],
+            dst_ref=down_out.at[recv_slot],
+            send_sem=d_send.at[g],
+            recv_sem=d_recv.at[recv_slot],
+            device_id=(g, me),
+            device_id_type=MESH,
+        )
+
+    def forward_copy(g, piece):
+        return pltpu.make_async_remote_copy(
+            src_ref=full_ref.at[gi, piece],
+            dst_ref=full_ref.at[gi, piece],
+            send_sem=f_send.at[g],
+            recv_sem=f_recv.at[gi],
+            device_id=(g, me),
+            device_id_type=MESH,
+        )
+
+    def whole_from(g):
+        return pltpu.make_async_remote_copy(
+            src_ref=full_ref.at[gi],
+            dst_ref=full_ref.at[g],
+            send_sem=f_send.at[g],
+            recv_sem=f_recv.at[g],
+            device_id=(g, me),
+            device_id_type=MESH,
+        )
+
+    barrier = pltpu.get_barrier_semaphore()
+
+    def greet(k, carry):
+        j = lax.rem(me + k, n_exp)
+        pl.semaphore_signal(barrier, 1, device_id=(gi, j), device_id_type=MESH)
+        return carry
+
+    lax.fori_loop(1, n_exp, greet, 0)
+    for k in range(1, n_dp):
+        g = lax.rem(gi + k, n_dp)
+        pl.semaphore_signal(barrier, 1, device_id=(g, me), device_id_type=MESH)
+    pl.semaphore_wait(barrier, n_exp - 1 + n_dp - 1)
+
+    def send_one(k, carry):
+        a2a_copy(lax.rem(me + k, n_exp), me).start()
+        return carry
+
+    lax.fori_loop(1, n_exp, send_one, 0)
+    local = pltpu.make_async_copy(send_ref.at[me], full_ref.at[gi, me], local_sem.at[0])
+    local.start()
+    for k in range(1, n_dp):
+        down_copy(lax.rem(gi + k, n_dp), gi).start()
+    own_cols = pl.ds(pl.multiple_of(gi * q, 128), q)
+    local_down = pltpu.make_async_copy(down_ref.at[:, :, own_cols], down_out.at[gi], local_sem.at[1])
+    local_down.start()
+
+    local.wait()
+    for k in range(1, n_dp):
+        forward_copy(lax.rem(gi + k, n_dp), me).start()
+
+    def take_one(k, carry):
+        j = lax.rem(me - k + n_exp, n_exp)
+        a2a_copy(j, j).wait_recv()
+        for step in range(1, n_dp):
+            forward_copy(lax.rem(gi + step, n_dp), j).start()
+        return carry
+
+    lax.fori_loop(1, n_exp, take_one, 0)
+
+    def sent_one(k, carry):
+        a2a_copy(lax.rem(me + k, n_exp), me).wait_send()
+        return carry
+
+    lax.fori_loop(1, n_exp, sent_one, 0)
+    for k in range(1, n_dp):
+        g = lax.rem(gi + k, n_dp)
+        down_copy(g, gi).wait_send()
+        down_copy(g, g).wait_recv()
+        whole_from(g).wait_send()
+        whole_from(g).wait_recv()
+    local_down.wait()
+
+
+def dispatch(send, down):
+    n_exp = lax.axis_size("expert")
+    n_dp = lax.axis_size("dp")
+    q = down.shape[-1] // n_dp
+    any_spec = pl.BlockSpec(memory_space=pl.ANY)
+    moved = send.size * send.dtype.itemsize * n_dp + down.size * down.dtype.itemsize
+    return pl.pallas_call(
+        functools.partial(dispatch_kernel, n_exp, n_dp),
+        out_shape=(
+            jax.ShapeDtypeStruct((n_dp,) + send.shape, send.dtype),
+            jax.ShapeDtypeStruct((n_dp,) + down.shape[:-1] + (q,), down.dtype),
+        ),
+        in_specs=[any_spec, any_spec],
+        out_specs=(any_spec, any_spec),
+        scratch_shapes=[
+            pltpu.SemaphoreType.DMA((n_exp,)),
+            pltpu.SemaphoreType.DMA((n_exp,)),
+            pltpu.SemaphoreType.DMA((n_dp,)),
+            pltpu.SemaphoreType.DMA((n_dp,)),
+            pltpu.SemaphoreType.DMA((n_dp,)),
+            pltpu.SemaphoreType.DMA((n_dp,)),
+            pltpu.SemaphoreType.DMA((2,)),
+        ],
+        compiler_params=pltpu.CompilerParams(collective_id=2, has_side_effects=True),
+        cost_estimate=pl.CostEstimate(flops=0, transcendentals=0, bytes_accessed=2 * moved),
+    )(send, down)
+
+
 def assign_slots(experts, replica_key, slot_expert):
     flat_experts = experts.reshape(-1)
     holders = (flat_experts[:, None] == slot_expert[None, :]).astype(jnp.int32)
@@ -131,12 +259,13 @@
     return jnp.sum(matched * numbers[None, :], axis=1)
 
 
-def slot_activated(flat_rows, gate_up_one):
-    model_width = flat_rows.shape[1]
+def slot_activated(quarters, gate_up_one):
+    group_count, _, quarter = quarters.shape
     unit_count = gate_up_one.shape[2]
-    gate_up_out = jnp.dot(
-        flat_rows,
-        gate_up_one.reshape(model_width, 2 * unit_count),
+    gate_up_out = lax.dot_general(
+        quarters,
+        gate_up_one.reshape(group_count, quarter, 2 * unit_count),
+        (((0, 2), (0, 1)), ((), ())),
         preferred_element_type=jnp.float32,
     )
     return (jax.nn.silu(gate_up_out[:, :unit_count]) * gate_up_out[:, unit_count:]).astype(
@@ -207,12 +336,11 @@
         .set(normed_part[source_rows])
     )
     outgoing = outgoing[:-1].reshape(peer_count, buffer_rows, quarter)
-    incoming_part, down_parts = exchange(outgoing, down_weight, collective_id=0)
-    incoming = lax.all_gather(incoming_part, "dp", axis=2, tiled=True)
-    flat_in = incoming.reshape(peer_count * buffer_rows, model_width)
-
-    first_act = slot_activated(flat_in, slot_gate_up_weight[0])
-    second_act = slot_activated(flat_in, slot_gate_up_weight[1])
+    full_in, down_parts = dispatch(outgoing, down_weight)
+    quarters = full_in.reshape(group_count, peer_count * buffer_rows, quarter)
+
+    first_act = slot_activated(quarters, slot_gate_up_weight[0])
+    second_act = slot_activated(quarters, slot_gate_up_weight[1])
     first_cap = lax.dynamic_index_in_dim(capacity, me * per_device, keepdims=False)
     row_index = jnp.arange(peer_count * buffer_rows, dtype=jnp.int32) % buffer_rows
     in_first = (row_index < first_cap)[:, None]

time: 270 us -> 268 us (level)
  waiting for transfers between devices: 99.4 us -> 34.3 us
  Pallas kernels: 90.4 us -> 147 us
  local copies, waits for them, and re-layouts: 34.5 us -> 41 us
    pallas_call x0 -> x1, Pallas kernels: none -> 102 us  [dispatch(): pl.pallas_call(functools.partial(dispatch_kernel, n_exp, n_dp), out_shape...]
    all_gather x1 -> x0, waiting for transfers between devices: 61.6 us -> none  [on_device(): incoming = lax.all_gather(incoming_part, 'dp', axis=2, tiled=True)]
    pallas_call x2 -> x1, Pallas kernels: 90.4 us -> 44.9 us  [exchange(): pl.pallas_call(functools.partial(exchange_kernel, n_exp, n_dp, with_down)...]
    another operation x3 -> x5, local copies, waits for them, and re-layouts: 0.28 us -> 7.33 us  [the longest x2 7.06 us: slot_activated(): gate_up_one.reshape(group_count, quarter, 2 * unit_count)]
    all_gather x1, waiting for transfers between devices: 37.7 us -> 34.3 us  [on_device(): act_all = lax.all_gather(act_here, 'dp', axis=1, tiled=True)]
  transfers between devices with their start and end apart: 2 -> 1, of which waited for: 2 -> 1; matrix products, arithmetic and copies ran while one was open for 6% -> 3% of each run, Pallas kernels for 0% -> 0%
where the time goes in v4:
time: 268 us; the launch traced here: 264 us
  Pallas kernels  147 us (55%)
  local copies, waits for them, and re-layouts  41 us (15%)
  waiting for transfers between devices  34.3 us (13%)
  matrix products  18.6 us (7%)
  between operations  13.8 us (5%)
  other arithmetic  9.18 us (3%)
    pallas_call x1, Pallas kernels, dispatch(): pl.pallas_call(functools.partial(dispatch_kernel, n_exp, n_dp), out_shape...  102 us
    pallas_call x1, Pallas kernels, exchange(): pl.pallas_call(functools.partial(exchange_kernel, n_exp, n_dp, with_down)...  44.9 us
    all_gather x1, waiting for transfers between devices, on_device(): act_all = lax.all_gather(act_here, 'dp', axis=1, tiled=True)  34.3 us
    scatter x1, local copies, waits for them, and re-layouts, on_device(): outgoing = jnp.zeros((peer_count * buffer_rows + 1, quarter), jnp.bfloat1...  10.3 us
    dot_general x8, matrix products, group_sums(): jnp.dot(act_all[:, lower:lower + unit_count], down_cols[lower:lower + uni...  9.22 us
    dot_general x2, matrix products, slot_activated(): lax.dot_general(quarters, gate_up_one.reshape(group_count, quarter, 2 * u...  9.06 us
    gather x5, local copies, waits for them, and re-layouts, on_device(): jnp.take_along_axis(logits, experts, axis=1)  7.34 us
    another operation x2, local copies, waits for them, and re-layouts, slot_activated(): gate_up_one.reshape(group_count, quarter, 2 * unit_count)  7.06 us
  transfers between devices with their start and end apart: 1, of which 1 were waited for; matrix products, arithmetic and copies ran while one was open for 3% of the time, Pallas kernels for 0%

profile of v4, /device:TPU:89, one launch (start us, length us, event | category | flops | bytes accessed | tf_op | source)
XLA Modules:
  0.0 263.9 jit_solution(17940252057613999305)
XLA Ops:
  6.6 0.8 copy.21
  7.5 0.8 convert_reduce_fusion
  8.3 0.8 compare_convert_fusion
  9.0 1.2 fusion.3
  10.3 1.2 dynamic_slice.11
  11.5 0.7 fusion.27
  12.2 0.7 convert_element_type.95
  12.9 0.8 copy.22
  15.8 10.3 %scatter_custom_fusion = bf16[1537,512]{1,0:T(8,128)(2,1)S(1)} fusion(s32[1024]{0:T(1024)S(1)} %bitcast.90, bf16[128,512]{1,0:T(8,128)(2,1)S(1)} %constant_dynamic-slice_fusion, s32[1024]{0:T(1024)S(1)} %broadcast_clamp_fusion.1, bf16[]{:T(256)} %constant.114.clone.1), kind=kCustom, calls=%fused_computation.26 | custom fusion | bytes 1573890 | tf_op jit(solution)/shard_map/scatter | solution.py:336
  26.1 1.3 slice.140
  27.4 5.7 %fusion.31 = (bf16[1,2048,2,256]{3,2,1,0:T(2,128)(2,1)}, bf16[1,2048,2,256]{3,2,1,0:T(2,128)(2,1)S(1)}) fusion(bf16[2,2048,2,256]{3,2,1,0:T(2,128)(2,1)} %param.16), kind=kLoop, calls=%fused_computation.94 | loop fusion | bytes 8388608 | tf_op jit(solution)/shard_map/slice | solution.py:343
  33.1 4.4 %reshape_squeeze.7 = bf16[4,512,512]{2,1,0:T(8,128)(2,1)} reshape(bf16[1,2048,2,256]{3,2,1,0:T(2,128)(2,1)} %get-tuple-element.11) | data formatting | bytes 4194304 | tf_op jit(solution)/shard_map/reshape;squeeze | solution.py:267
  37.5 2.6 reshape_squeeze.6
  40.1 102.2 %shard_map.91 = (bf16[4,64,24,512]{3,2,1,0:T(8,128)(2,1)}, bf16[4,2,256,512]{3,2,1,0:T(8,128)(2,1)}) custom-call(bf16[64,24,512]{2,1,0:T(8,128)(2,1)} %bitcast.73, bf16[2,256,2048]{2,1,0:T(8,128)(2,1)} %down_ref.1), custom_call_target="tpu_custom_call" | custom-call | bytes 16777216 | tf_op jit(solution)/shard_map/pallas_call | solution.py:229
  142.4 5.6 %convolution_bitcast_fusion = f32[1536,512]{1,0:T(8,128)S(1)} fusion(bf16[4,1536,512]{2,1,0:T(8,128)(2,1)} %bitcast.92, bf16[4,512,512]{2,1,0:T(8,128)(2,1)S(1)} %copy-done.4), kind=kOutput, calls=%fused_computation.4 | convolution fusion | flops 3221225472 | bytes 11534336 | tf_op jit(solution)/shard_map/dot_general | solution.py:265
  148.0 3.4 %convolution_bitcast_fusion.1 = f32[1536,512]{1,0:T(8,128)S(1)} fusion(bf16[4,1536,512]{2,1,0:T(8,128)(2,1)S(1)} %bitcast.93, bf16[4,512,512]{2,1,0:T(8,128)(2,1)S(1)} %copy-done.5), kind=kOutput, calls=%fused_computation.5 | convolution fusion | flops 3221225472 | bytes 11534336 | tf_op jit(solution)/shard_map/dot_general | solution.py:265
  151.5 2.1 fusion.9
  154.2 7.0 %gather_fusion.1 = f32[1024]{0:T(1024)S(1)} fusion(f32[128,64]{0,1:T(8,128)S(1)} %fusion.32, s32[1024]{0:T(1024)S(1)} %reshape.287), kind=kCustom, calls=%fused_computation.2 | custom fusion | bytes 16384 | tf_op jit(solution)/shard_map/jit(take_along_axis)/gather | solution.py:316
  161.7 34.3 %all-gather.2.cloned.1.call-done = bf16[1536,1024]{1,0:T(8,128)(2,1)} async-done(((bf16[1536,256]{1,0:T(8,128)(2,1)}), bf16[1536,1024]{1,0:T(8,128)(2,1)}) %all-gather.2.cloned.1.call-update) | async-done | bytes 3145744 | tf_op jit(solution)/shard_map/all_gather | solution.py:348
  196.0 1.8 convolution_convert_fusion.3
  197.8 1.7 convolution_convert_fusion.2
  199.5 0.6 convolution_convert_fusion.1
  200.1 0.6 convolution_convert_fusion
  200.7 0.6 convolution_convert_fusion.4
  201.3 0.6 convolution_convert_fusion.5
  201.8 0.6 convolution_convert_fusion.6
  202.4 2.8 %select_convert_fusion = bf16[1536,512]{1,0:T(8,128)(2,1)} fusion(bf16[1536,512]{1,0:T(8,128)(2,1)S(1)} %convolution_convert_fusion, bf16[1536,512]{1,0:T(8,128)(2,1)S(1)} %convolution_convert_fusion.1, bf16[1536,512]{1,0:T(8,128)(2,1)S(1)} %convolution_convert_fusion.2, bf16[1536,512]{1,0:T(8,128)(2,1)S(1)} %convolution_convert_fusion.3, ...), kind=kOutput, calls=%fused_computation.6 | convolution fusion | flops 416022528 | bytes 13633536 | tf_op jit(solution)/shard_map/dot_general | solution.py:279
  205.2 44.9 %shard_map.92 = bf16[64,24,512]{2,1,0:T(8,128)(2,1)} custom-call(bf16[64,24,512]{2,1,0:T(8,128)(2,1)} %bitcast.75), custom_call_target="tpu_custom_call" | custom-call | bytes 3145728 | tf_op jit(solution)/shard_map/pallas_call | solution.py:112
  250.2 1.5 concatenate.3
  251.7 4.0 %gather_fusion = bf16[1024,512]{1,0:T(8,128)(2,1)S(1)} fusion(bf16[1537,512]{1,0:T(8,128)(2,1)S(1)} %concatenate.3, s32[1024]{0:T(1024)S(1)} %broadcast_clamp_fusion), kind=kCustom, calls=%fused_computation.1 | custom fusion | bytes 2101248 | tf_op jit(solution)/shard_map/gather | solution.py:360
  255.6 0.7 fusion
  256.4 0.7 add_convert_fusion
  (53 shorter events, 3.1 us)
Async XLA Ops:
  6.5 147.3 %copy-start = (bf16[2048,64]{0,1:T(8,128)(2,1)S(1)}, bf16[2048,64]{0,1:T(8,128)(2,1)}, u32[]{:S(2)}) copy-start(bf16[2048,64]{0,1:T(8,128)(2,1)} %param.11) | copy-start | bytes 786436
  6.5 7.9 %copy-start.7 = (s32[128]{0:T(128)S(1)}, s32[128]{0:T(128)}, u32[]{:S(2)}) copy-start(s32[128]{0:T(128)} %param.14) | copy-start | bytes 1540
  6.5 189.4 %all-gather.2.cloned.1.call-start = ((), (), s32[]{:S(2)}) async-start(), calls=%async_computation | async-start | bytes 3932160 | tf_op jit(solution)/shard_map/all_gather | solution.py:348
  13.8 1.5 copy-start.8
  14.3 1.2 copy-start.2
  40.1 102.2 %copy-start.4 = (bf16[4,512,512]{2,1,0:T(8,128)(2,1)S(1)}, bf16[4,512,512]{2,1,0:T(8,128)(2,1)}, u32[]{:S(2)}) copy-start(bf16[4,512,512]{2,1,0:T(8,128)(2,1)} %reshape_squeeze.7) | copy-start | bytes 6291460
  142.4 5.7 %copy-start.5 = (bf16[4,512,512]{2,1,0:T(8,128)(2,1)S(1)}, bf16[4,512,512]{2,1,0:T(8,128)(2,1)}, u32[]{:S(2)}) copy-start(bf16[4,512,512]{2,1,0:T(8,128)(2,1)} %reshape_squeeze.6) | copy-start | bytes 6291460
  142.4 5.7 %copy-start.9 = (bf16[4,64,24,512]{3,2,1,0:T(8,128)(2,1)S(1)}, bf16[4,64,24,512]{3,2,1,0:T(8,128)(2,1)}, u32[]{:S(2)}) copy-start(bf16[4,64,24,512]{3,2,1,0:T(8,128)(2,1)} %get-tuple-element.7) | copy-start | bytes 18874372
  151.5 2.1 copy-start.6
  154.2 41.8 %copy-start.3 = (bf16[4,2,256,512]{3,2,1,0:T(8,128)(2,1)S(1)}, bf16[4,2,256,512]{3,2,1,0:T(8,128)(2,1)}, u32[]{:S(2)}) copy-start(bf16[4,2,256,512]{3,2,1,0:T(8,128)(2,1)} %get-tuple-element.8) | copy-start | bytes 6291460
  196.0 3.6 %copy-start.1 = (bf16[1536,1024]{1,0:T(8,128)(2,1)S(1)}, bf16[1536,1024]{1,0:T(8,128)(2,1)}, u32[]{:S(2)}) copy-start(bf16[1536,1024]{1,0:T(8,128)(2,1)} %all-gather.2.cloned.1.call-done) | copy-start | bytes 9437188
Sparse Core Ops, SparseCore 0:
  153.7 42.1 all-gather.1

commit v5 on v4

--- a/solution.py
+++ b/solution.py
@@ -11,6 +11,7 @@
 
 CAPACITY_HIGH = 16
 CAP_DEV = 24
+SEND_WINDOW = 8
 
 
 def exchange_kernel(n_exp, n_dp, with_down, *refs):
@@ -180,11 +181,9 @@
         pl.semaphore_signal(barrier, 1, device_id=(g, me), device_id_type=MESH)
     pl.semaphore_wait(barrier, n_exp - 1 + n_dp - 1)
 
-    def send_one(k, carry):
+    window = min(SEND_WINDOW, n_exp - 1)
+    for k in range(1, window + 1):
         a2a_copy(lax.rem(me + k, n_exp), me).start()
-        return carry
-
-    lax.fori_loop(1, n_exp, send_one, 0)
     local = pltpu.make_async_copy(send_ref.at[me], full_ref.at[gi, me], local_sem.at[0])
     local.start()
     for k in range(1, n_dp):
@@ -202,6 +201,11 @@
         a2a_copy(j, j).wait_recv()
         for step in range(1, n_dp):
             forward_copy(lax.rem(gi + step, n_dp), j).start()
+
+        @pl.when(k + window < n_exp)
+        def _():
+            a2a_copy(lax.rem(me + k + window, n_exp), me).start()
+
         return carry
 
     lax.fori_loop(1, n_exp, take_one, 0)
@@ -248,6 +252,54 @@
     )(send, down)
 
 
+def gather_kernel(n_dp, src_ref, out_ref, send_sem, recv_sem, local_sem):
+    me = lax.axis_index("expert")
+    gi = lax.axis_index("dp")
+
+    def copy_to(g, recv_slot):
+        return pltpu.make_async_remote_copy(
+            src_ref=src_ref,
+            dst_ref=out_ref.at[recv_slot],
+            send_sem=send_sem.at[g],
+            recv_sem=recv_sem.at[recv_slot],
+            device_id=(g, me),
+            device_id_type=MESH,
+        )
+
+    barrier = pltpu.get_barrier_semaphore()
+    for k in range(1, n_dp):
+        pl.semaphore_signal(barrier, 1, device_id=(lax.rem(gi + k, n_dp), me), device_id_type=MESH)
+    pl.semaphore_wait(barrier, n_dp - 1)
+    for k in range(1, n_dp):
+        copy_to(lax.rem(gi + k, n_dp), gi).start()
+    local = pltpu.make_async_copy(src_ref, out_ref.at[gi], local_sem.at[0])
+    local.start()
+    for k in range(1, n_dp):
+        g = lax.rem(gi + k, n_dp)
+        copy_to(g, gi).wait_send()
+        copy_to(g, g).wait_recv()
+    local.wait()
+
+
+def gather_dp(src):
+    n_dp = lax.axis_size("dp")
+    any_spec = pl.BlockSpec(memory_space=pl.ANY)
+    moved = src.size * src.dtype.itemsize * n_dp
+    return pl.pallas_call(
+        functools.partial(gather_kernel, n_dp),
+        out_shape=jax.ShapeDtypeStruct((n_dp,) + src.shape, src.dtype),
+        in_specs=[any_spec],
+        out_specs=any_spec,
+        scratch_shapes=[
+            pltpu.SemaphoreType.DMA((n_dp,)),
+            pltpu.SemaphoreType.DMA((n_dp,)),
+            pltpu.SemaphoreType.DMA((1,)),
+        ],
+        compiler_params=pltpu.CompilerParams(collective_id=3, has_side_effects=True),
+        cost_estimate=pl.CostEstimate(flops=0, transcendentals=0, bytes_accessed=2 * moved),
+    )(src)
+
+
 def assign_slots(experts, replica_key, slot_expert):
     flat_experts = experts.reshape(-1)
     holders = (flat_experts[:, None] == slot_expert[None, :]).astype(jnp.int32)
@@ -275,9 +327,10 @@
 
 def group_sums(act_all, down_cols, unit_count):
     total = None
-    for lower in range(0, act_all.shape[1], unit_count):
+    for group in range(act_all.shape[0]):
+        lower = group * unit_count
         piece = jnp.dot(
-            act_all[:, lower:lower + unit_count],
+            act_all[group],
             down_cols[lower:lower + unit_count],
             preferred_element_type=jnp.float32,
         )
@@ -345,7 +398,7 @@
     row_index = jnp.arange(peer_count * buffer_rows, dtype=jnp.int32) % buffer_rows
     in_first = (row_index < first_cap)[:, None]
     act_here = jnp.where(in_first, first_act, second_act)
-    act_all = lax.all_gather(act_here, "dp", axis=1, tiled=True)
+    act_all = gather_dp(act_here)
     down_here = jnp.swapaxes(down_parts, 0, 1).reshape(per_device, -1, quarter)
     unit_count = down_weight.shape[1]
     first_sum = group_sums(act_all, down_here[0], unit_count)

time: 268 us -> 260 us (0.970)
  the two profiles are of different devices: /device:TPU:89 before, /device:TPU:1 now
where the time goes in v5:
time: 260 us; the launch traced here: 259 us
  Pallas kernels  188 us (72%)
  local copies, waits for them, and re-layouts  40.9 us (16%)
  matrix products  18.6 us (7%)
  other arithmetic  11.2 us (4%)
    pallas_call x1, Pallas kernels, dispatch(): pl.pallas_call(functools.partial(dispatch_kernel, n_exp, n_dp), out_shape...  106 us
    pallas_call x1, Pallas kernels, exchange(): pl.pallas_call(functools.partial(exchange_kernel, n_exp, n_dp, with_down)...  45.3 us
    pallas_call x1, Pallas kernels, gather_dp(): pl.pallas_call(functools.partial(gather_kernel, n_dp), out_shape=jax.Shap...  36.8 us
    scatter x1, local copies, waits for them, and re-layouts, on_device(): outgoing = jnp.zeros((peer_count * buffer_rows + 1, quarter), jnp.bfloat1...  10.3 us
    dot_general x8, matrix products, group_sums(): jnp.dot(act_all[group], down_cols[lower:lower + unit_count], preferred_el...  9.24 us
    dot_general x2, matrix products, slot_activated(): lax.dot_general(quarters, gate_up_one.reshape(group_count, quarter, 2 * u...  9.08 us
    gather x5, local copies, waits for them, and re-layouts, on_device(): jnp.take_along_axis(logits, experts, axis=1)  7.34 us
    another operation x2, local copies, waits for them, and re-layouts, slot_activated(): gate_up_one.reshape(group_count, quarter, 2 * unit_count)  7.06 us

profile of v5, /device:TPU:1, one launch (start us, length us, event | category | flops | bytes accessed | tf_op | source)
XLA Modules:
  0.0 259.3 jit_solution(698856041681476256)
XLA Ops:
  0.0 1.3 dynamic_slice.11
  1.3 1.2 fusion.3
  2.5 0.7 fusion.35
  3.2 0.7 bitcast_or_fusion
  3.9 0.7 convert_element_type.95
  4.8 0.8 copy.22
  5.7 0.8 copy.21
  6.6 0.8 convert_reduce_fusion
  7.5 1.2 fusion.5
  9.1 7.0 %gather_fusion.1 = f32[1024]{0:T(1024)S(1)} fusion(f32[128,64]{0,1:T(8,128)S(1)} %fusion.40, s32[1024]{0:T(1024)S(1)} %reshape.287), kind=kCustom, calls=%fused_computation.2 | custom fusion | bytes 16384 | tf_op jit(solution)/shard_map/jit(take_along_axis)/gather | solution.py:369
  18.3 10.3 %scatter_custom_fusion = bf16[1537,512]{1,0:T(8,128)(2,1)S(1)} fusion(s32[1024]{0:T(1024)S(1)} %bitcast.111, bf16[128,512]{1,0:T(8,128)(2,1)S(1)} %constant_dynamic-slice_fusion, s32[1024]{0:T(1024)S(1)} %broadcast_clamp_fusion.1, bf16[]{:T(256)} %constant.114.clone.1), kind=kCustom, calls=%fused_computation.26 | custom fusion | bytes 1573890 | tf_op jit(solution)/shard_map/scatter | solution.py:389
  28.7 1.3 slice.140
  30.0 5.7 %fusion.39 = (bf16[1,2048,2,256]{3,2,1,0:T(2,128)(2,1)}, bf16[1,2048,2,256]{3,2,1,0:T(2,128)(2,1)S(1)}) fusion(bf16[2,2048,2,256]{3,2,1,0:T(2,128)(2,1)} %param.16), kind=kLoop, calls=%fused_computation.102 | loop fusion | bytes 8388608 | tf_op jit(solution)/shard_map/slice | solution.py:396
  35.6 4.4 %reshape_squeeze.7 = bf16[4,512,512]{2,1,0:T(8,128)(2,1)} reshape(bf16[1,2048,2,256]{3,2,1,0:T(2,128)(2,1)} %get-tuple-element.11) | data formatting | bytes 4194304 | tf_op jit(solution)/shard_map/reshape;squeeze | solution.py:319
  40.1 2.6 %reshape_squeeze.6 = bf16[4,512,512]{2,1,0:T(8,128)(2,1)} reshape(bf16[1,2048,2,256]{3,2,1,0:T(2,128)(2,1)S(1)} %get-tuple-element.12) | data formatting | bytes 4194304 | tf_op jit(solution)/shard_map/reshape;squeeze | solution.py:319
  42.7 106.2 %shard_map.91 = (bf16[4,64,24,512]{3,2,1,0:T(8,128)(2,1)}, bf16[4,2,256,512]{3,2,1,0:T(8,128)(2,1)}) custom-call(bf16[64,24,512]{2,1,0:T(8,128)(2,1)} %bitcast.93, bf16[2,256,2048]{2,1,0:T(8,128)(2,1)} %down_ref.1), custom_call_target="tpu_custom_call" | custom-call | bytes 16777216 | tf_op jit(solution)/shard_map/pallas_call | solution.py:233
  148.9 5.6 %convolution_bitcast_fusion = f32[1536,512]{1,0:T(8,128)S(1)} fusion(bf16[4,1536,512]{2,1,0:T(8,128)(2,1)} %bitcast.112, bf16[4,512,512]{2,1,0:T(8,128)(2,1)S(1)} %copy-done.3), kind=kOutput, calls=%fused_computation.4 | convolution fusion | flops 3221225472 | bytes 11534336 | tf_op jit(solution)/shard_map/dot_general | solution.py:317
  154.6 3.4 %convolution_bitcast_fusion.1 = f32[1536,512]{1,0:T(8,128)S(1)} fusion(bf16[4,1536,512]{2,1,0:T(8,128)(2,1)S(1)} %bitcast.113, bf16[4,512,512]{2,1,0:T(8,128)(2,1)S(1)} %copy-done.4), kind=kOutput, calls=%fused_computation.5 | convolution fusion | flops 3221225472 | bytes 11534336 | tf_op jit(solution)/shard_map/dot_general | solution.py:317
  158.0 2.1 fusion.17.src_ref
  160.1 36.8 %shard_map.92 = bf16[4,1536,256]{2,1,0:T(8,128)(2,1)} custom-call(bf16[1536,256]{1,0:T(8,128)(2,1)} %fusion.17.src_ref), custom_call_target="tpu_custom_call" | custom-call | bytes 6291456 | tf_op jit(solution)/shard_map/pallas_call | solution.py:288
  197.0 1.8 convolution_convert_fusion.3
  198.8 1.7 convolution_convert_fusion.2
  200.5 0.6 convolution_convert_fusion.1
  201.1 0.6 convolution_convert_fusion
  201.7 0.6 convolution_convert_fusion.4
  202.8 0.6 convolution_convert_fusion.6
  203.4 2.9 %select_convert_fusion = bf16[1536,512]{1,0:T(8,128)(2,1)} fusion(bf16[1536,512]{1,0:T(8,128)(2,1)S(1)} %convolution_convert_fusion, bf16[1536,512]{1,0:T(8,128)(2,1)S(1)} %convolution_convert_fusion.1, bf16[1536,512]{1,0:T(8,128)(2,1)S(1)} %convolution_convert_fusion.2, bf16[1536,512]{1,0:T(8,128)(2,1)S(1)} %convolution_convert_fusion.3, ...), kind=kOutput, calls=%fused_computation.6 | convolution fusion | flops 416022528 | bytes 13633536 | tf_op jit(solution)/shard_map/dot_general | solution.py:332
  206.2 45.3 %shard_map.93 = bf16[64,24,512]{2,1,0:T(8,128)(2,1)} custom-call(bf16[64,24,512]{2,1,0:T(8,128)(2,1)} %bitcast.95), custom_call_target="tpu_custom_call" | custom-call | bytes 3145728 | tf_op jit(solution)/shard_map/pallas_call | solution.py:113
  251.5 1.5 concatenate.3
  253.0 4.0 %gather_fusion = bf16[1024,512]{1,0:T(8,128)(2,1)S(1)} fusion(bf16[1537,512]{1,0:T(8,128)(2,1)S(1)} %concatenate.3, s32[1024]{0:T(1024)S(1)} %broadcast_clamp_fusion), kind=kCustom, calls=%fused_computation.1 | custom fusion | bytes 2101248 | tf_op jit(solution)/shard_map/gather | solution.py:413
  257.0 0.7 fusion
  257.7 1.6 add_convert_fusion
  (49 shorter events, 3.6 us)
Async XLA Ops:
  0.0 8.7 %copy-start = (bf16[2048,64]{0,1:T(8,128)(2,1)S(1)}, bf16[2048,64]{0,1:T(8,128)(2,1)}, u32[]{:S(2)}) copy-start(bf16[2048,64]{0,1:T(8,128)(2,1)} %param.11) | copy-start | bytes 786436
  9.0 7.2 %copy-start.6 = (s32[128]{0:T(128)S(1)}, s32[128]{0:T(128)}, u32[]{:S(2)}) copy-start(s32[128]{0:T(128)} %param.14) | copy-start | bytes 1540
  16.4 1.4 copy-start.7
  16.9 1.3 copy-start.5
  42.7 106.2 %copy-start.3 = (bf16[4,512,512]{2,1,0:T(8,128)(2,1)S(1)}, bf16[4,512,512]{2,1,0:T(8,128)(2,1)}, u32[]{:S(2)}) copy-start(bf16[4,512,512]{2,1,0:T(8,128)(2,1)} %reshape_squeeze.7) | copy-start | bytes 6291460
  148.9 5.7 %copy-start.4 = (bf16[4,512,512]{2,1,0:T(8,128)(2,1)S(1)}, bf16[4,512,512]{2,1,0:T(8,128)(2,1)}, u32[]{:S(2)}) copy-start(bf16[4,512,512]{2,1,0:T(8,128)(2,1)} %reshape_squeeze.6) | copy-start | bytes 6291460
  148.9 5.7 %copy-start.8 = (bf16[4,64,24,512]{3,2,1,0:T(8,128)(2,1)S(1)}, bf16[4,64,24,512]{3,2,1,0:T(8,128)(2,1)}, u32[]{:S(2)}) copy-start(bf16[4,64,24,512]{3,2,1,0:T(8,128)(2,1)} %get-tuple-element.7) | copy-start | bytes 18874372
  160.1 36.8 %copy-start.2 = (bf16[4,2,256,512]{3,2,1,0:T(8,128)(2,1)S(1)}, bf16[4,2,256,512]{3,2,1,0:T(8,128)(2,1)}, u32[]{:S(2)}) copy-start(bf16[4,2,256,512]{3,2,1,0:T(8,128)(2,1)} %get-tuple-element.8) | copy-start | bytes 6291460
  196.9 3.6 %copy-start.1 = (bf16[4,1536,256]{2,1,0:T(8,128)(2,1)S(1)}, bf16[4,1536,256]{2,1,0:T(8,128)(2,1)}, u32[]{:S(2)}) copy-start(bf16[4,1536,256]{2,1,0:T(8,128)(2,1)} %shard_map.92) | copy-start | bytes 9437188

commit v6 on v5

--- a/solution.py
+++ b/solution.py
@@ -122,10 +122,17 @@
 
 
 def dispatch_kernel(n_exp, n_dp, send_ref, down_ref, full_ref, down_out,
-                    a_send, a_recv, d_send, d_recv, f_send, f_recv, local_sem):
+                    a_send, a_recv, d_send, d_recv, n_send, lo_recv, hi_recv,
+                    r_send, r_recv, local_sem):
     me = lax.axis_index("expert")
     gi = lax.axis_index("dp")
     q = down_out.shape[-1]
+    half = full_ref.shape[-1] // 2
+    lo = lax.rem(gi + n_dp - 1, n_dp)
+    hi = lax.rem(gi + 1, n_dp)
+    far = lax.rem(gi + 2, n_dp)
+    first = pl.ds(0, half)
+    second = pl.ds(half, half)
 
     def a2a_copy(j, recv_slot):
         return pltpu.make_async_remote_copy(
@@ -148,23 +155,63 @@
             device_id_type=MESH,
         )
 
-    def forward_copy(g, piece):
+    def to_hi(piece):
         return pltpu.make_async_remote_copy(
             src_ref=full_ref.at[gi, piece],
             dst_ref=full_ref.at[gi, piece],
-            send_sem=f_send.at[g],
-            recv_sem=f_recv.at[gi],
-            device_id=(g, me),
-            device_id_type=MESH,
-        )
-
-    def whole_from(g):
-        return pltpu.make_async_remote_copy(
-            src_ref=full_ref.at[gi],
-            dst_ref=full_ref.at[g],
-            send_sem=f_send.at[g],
-            recv_sem=f_recv.at[g],
-            device_id=(g, me),
+            send_sem=n_send.at[1],
+            recv_sem=lo_recv.at[piece],
+            device_id=(hi, me),
+            device_id_type=MESH,
+        )
+
+    def to_lo(piece):
+        return pltpu.make_async_remote_copy(
+            src_ref=full_ref.at[gi, piece],
+            dst_ref=full_ref.at[gi, piece],
+            send_sem=n_send.at[0],
+            recv_sem=hi_recv.at[piece],
+            device_id=(lo, me),
+            device_id_type=MESH,
+        )
+
+    def from_lo(piece):
+        return pltpu.make_async_remote_copy(
+            src_ref=full_ref.at[lo, piece],
+            dst_ref=full_ref.at[lo, piece],
+            send_sem=n_send.at[0],
+            recv_sem=lo_recv.at[piece],
+            device_id=(lo, me),
+            device_id_type=MESH,
+        )
+
+    def from_hi(piece):
+        return pltpu.make_async_remote_copy(
+            src_ref=full_ref.at[hi, piece],
+            dst_ref=full_ref.at[hi, piece],
+            send_sem=n_send.at[1],
+            recv_sem=hi_recv.at[piece],
+            device_id=(hi, me),
+            device_id_type=MESH,
+        )
+
+    def relay_up(piece):
+        return pltpu.make_async_remote_copy(
+            src_ref=full_ref.at[lo, piece, :, first],
+            dst_ref=full_ref.at[lo, piece, :, first],
+            send_sem=r_send.at[1],
+            recv_sem=r_recv.at[0],
+            device_id=(hi, me),
+            device_id_type=MESH,
+        )
+
+    def relay_down(piece):
+        return pltpu.make_async_remote_copy(
+            src_ref=full_ref.at[hi, piece, :, second],
+            dst_ref=full_ref.at[hi, piece, :, second],
+            send_sem=r_send.at[0],
+            recv_sem=r_recv.at[1],
+            device_id=(lo, me),
             device_id_type=MESH,
         )
 
@@ -193,14 +240,14 @@
     local_down.start()
 
     local.wait()
-    for k in range(1, n_dp):
-        forward_copy(lax.rem(gi + k, n_dp), me).start()
+    to_hi(me).start()
+    to_lo(me).start()
 
     def take_one(k, carry):
         j = lax.rem(me - k + n_exp, n_exp)
         a2a_copy(j, j).wait_recv()
-        for step in range(1, n_dp):
-            forward_copy(lax.rem(gi + step, n_dp), j).start()
+        to_hi(j).start()
+        to_lo(j).start()
 
         @pl.when(k + window < n_exp)
         def _():
@@ -209,6 +256,16 @@
         return carry
 
     lax.fori_loop(1, n_exp, take_one, 0)
+
+    def relay_one(k, carry):
+        j = lax.rem(me - k + n_exp, n_exp)
+        from_lo(j).wait_recv()
+        relay_up(j).start()
+        from_hi(j).wait_recv()
+        relay_down(j).start()
+        return carry
+
+    lax.fori_loop(0, n_exp, relay_one, 0)
 
     def sent_one(k, carry):
         a2a_copy(lax.rem(me + k, n_exp), me).wait_send()
@@ -219,9 +276,31 @@
         g = lax.rem(gi + k, n_dp)
         down_copy(g, gi).wait_send()
         down_copy(g, g).wait_recv()
-        whole_from(g).wait_send()
-        whole_from(g).wait_recv()
     local_down.wait()
+    pltpu.make_async_remote_copy(
+        src_ref=full_ref.at[gi], dst_ref=full_ref.at[gi], send_sem=n_send.at[1],
+        recv_sem=lo_recv.at[0], device_id=(hi, me), device_id_type=MESH,
+    ).wait_send()
+    pltpu.make_async_remote_copy(
+        src_ref=full_ref.at[gi], dst_ref=full_ref.at[gi], send_sem=n_send.at[0],
+        recv_sem=hi_recv.at[0], device_id=(lo, me), device_id_type=MESH,
+    ).wait_send()
+    pltpu.make_async_remote_copy(
+        src_ref=full_ref.at[lo, :, :, first], dst_ref=full_ref.at[lo, :, :, first],
+        send_sem=r_send.at[1], recv_sem=r_recv.at[0], device_id=(hi, me), device_id_type=MESH,
+    ).wait_send()
+    pltpu.make_async_remote_copy(
+        src_ref=full_ref.at[hi, :, :, second], dst_ref=full_ref.at[hi, :, :, second],
+        send_sem=r_send.at[0], recv_sem=r_recv.at[1], device_id=(lo, me), device_id_type=MESH,
+    ).wait_send()
+    pltpu.make_async_remote_copy(
+        src_ref=full_ref.at[far, :, :, first], dst_ref=full_ref.at[far, :, :, first],
+        send_sem=r_send.at[1], recv_sem=r_recv.at[0], device_id=(hi, me), device_id_type=MESH,
+    ).wait_recv()
+    pltpu.make_async_remote_copy(
+        src_ref=full_ref.at[far, :, :, second], dst_ref=full_ref.at[far, :, :, second],
+        send_sem=r_send.at[0], recv_sem=r_recv.at[1], device_id=(lo, me), device_id_type=MESH,
+    ).wait_recv()
 
 
 def dispatch(send, down):
@@ -243,8 +322,11 @@
             pltpu.SemaphoreType.DMA((n_exp,)),
             pltpu.SemaphoreType.DMA((n_dp,)),
             pltpu.SemaphoreType.DMA((n_dp,)),
-            pltpu.SemaphoreType.DMA((n_dp,)),
-            pltpu.SemaphoreType.DMA((n_dp,)),
+            pltpu.SemaphoreType.DMA((2,)),
+            pltpu.SemaphoreType.DMA((n_exp,)),
+            pltpu.SemaphoreType.DMA((n_exp,)),
+            pltpu.SemaphoreType.DMA((2,)),
+            pltpu.SemaphoreType.DMA((2,)),
             pltpu.SemaphoreType.DMA((2,)),
         ],
         compiler_params=pltpu.CompilerParams(collective_id=2, has_side_effects=True),

time: 260 us -> 244 us (0.938)
  the two profiles are of different devices: /device:TPU:1 before, /device:TPU:89 now
where the time goes in v6:
time: 244 us; the launch traced here: 240 us
  Pallas kernels  169 us (69%)
  local copies, waits for them, and re-layouts  40.9 us (17%)
  matrix products  18.6 us (8%)
  other arithmetic  11.2 us (5%)
    pallas_call x1, Pallas kernels, dispatch(): pl.pallas_call(functools.partial(dispatch_kernel, n_exp, n_dp), out_shape...  86.5 us
    pallas_call x1, Pallas kernels, exchange(): pl.pallas_call(functools.partial(exchange_kernel, n_exp, n_dp, with_down)...  46 us
    pallas_call x1, Pallas kernels, gather_dp(): pl.pallas_call(functools.partial(gather_kernel, n_dp), out_shape=jax.Shap...  36.9 us
    scatter x1, local copies, waits for them, and re-layouts, on_device(): outgoing = jnp.zeros((peer_count * buffer_rows + 1, quarter), jnp.bfloat1...  10.3 us
    dot_general x8, matrix products, group_sums(): jnp.dot(act_all[group], down_cols[lower:lower + unit_count], preferred_el...  9.24 us
    dot_general x2, matrix products, slot_activated(): lax.dot_general(quarters, gate_up_one.reshape(group_count, quarter, 2 * u...  9.07 us
    gather x5, local copies, waits for them, and re-layouts, on_device(): jnp.take_along_axis(logits, experts, axis=1)  7.34 us
    another operation x2, local copies, waits for them, and re-layouts, slot_activated(): gate_up_one.reshape(group_count, quarter, 2 * unit_count)  7.06 us

profile of v6, /device:TPU:89, one launch (start us, length us, event | category | flops | bytes accessed | tf_op | source)
XLA Modules:
  0.0 240.4 jit_solution(11101304390549715217)
XLA Ops:
  0.0 1.3 dynamic_slice.11
  1.3 1.2 fusion.3
  2.5 0.7 fusion.35
  3.2 0.7 bitcast_or_fusion
  3.9 0.7 convert_element_type.95
  4.8 0.8 copy.22
  5.7 0.8 copy.21
  6.6 0.8 convert_reduce_fusion
  7.5 1.2 fusion.5
  9.1 7.0 %gather_fusion.1 = f32[1024]{0:T(1024)S(1)} fusion(f32[128,64]{0,1:T(8,128)S(1)} %fusion.40, s32[1024]{0:T(1024)S(1)} %reshape.287), kind=kCustom, calls=%fused_computation.2 | custom fusion | bytes 16384 | tf_op jit(solution)/shard_map/jit(take_along_axis)/gather | solution.py:451
  18.3 10.3 %scatter_custom_fusion = bf16[1537,512]{1,0:T(8,128)(2,1)S(1)} fusion(s32[1024]{0:T(1024)S(1)} %bitcast.111, bf16[128,512]{1,0:T(8,128)(2,1)S(1)} %constant_dynamic-slice_fusion, s32[1024]{0:T(1024)S(1)} %broadcast_clamp_fusion.1, bf16[]{:T(256)} %constant.114.clone.1), kind=kCustom, calls=%fused_computation.26 | custom fusion | bytes 1573890 | tf_op jit(solution)/shard_map/scatter | solution.py:471
  28.7 1.3 slice.140
  30.0 5.7 %fusion.39 = (bf16[1,2048,2,256]{3,2,1,0:T(2,128)(2,1)}, bf16[1,2048,2,256]{3,2,1,0:T(2,128)(2,1)S(1)}) fusion(bf16[2,2048,2,256]{3,2,1,0:T(2,128)(2,1)} %param.16), kind=kLoop, calls=%fused_computation.102 | loop fusion | bytes 8388608 | tf_op jit(solution)/shard_map/slice | solution.py:478
  35.6 4.4 %reshape_squeeze.7 = bf16[4,512,512]{2,1,0:T(8,128)(2,1)} reshape(bf16[1,2048,2,256]{3,2,1,0:T(2,128)(2,1)} %get-tuple-element.11) | data formatting | bytes 4194304 | tf_op jit(solution)/shard_map/reshape;squeeze | solution.py:401
  40.1 2.6 %reshape_squeeze.6 = bf16[4,512,512]{2,1,0:T(8,128)(2,1)} reshape(bf16[1,2048,2,256]{3,2,1,0:T(2,128)(2,1)S(1)} %get-tuple-element.12) | data formatting | bytes 4194304 | tf_op jit(solution)/shard_map/reshape;squeeze | solution.py:401
  42.7 86.5 %shard_map.91 = (bf16[4,64,24,512]{3,2,1,0:T(8,128)(2,1)}, bf16[4,2,256,512]{3,2,1,0:T(8,128)(2,1)}) custom-call(bf16[64,24,512]{2,1,0:T(8,128)(2,1)} %bitcast.93, bf16[2,256,2048]{2,1,0:T(8,128)(2,1)} %down_ref.1), custom_call_target="tpu_custom_call" | custom-call | bytes 16777216 | tf_op jit(solution)/shard_map/pallas_call | solution.py:312
  129.2 5.6 %convolution_bitcast_fusion = f32[1536,512]{1,0:T(8,128)S(1)} fusion(bf16[4,1536,512]{2,1,0:T(8,128)(2,1)} %bitcast.112, bf16[4,512,512]{2,1,0:T(8,128)(2,1)S(1)} %copy-done.3), kind=kOutput, calls=%fused_computation.4 | convolution fusion | flops 3221225472 | bytes 11534336 | tf_op jit(solution)/shard_map/dot_general | solution.py:399
  134.9 3.4 %convolution_bitcast_fusion.1 = f32[1536,512]{1,0:T(8,128)S(1)} fusion(bf16[4,1536,512]{2,1,0:T(8,128)(2,1)S(1)} %bitcast.113, bf16[4,512,512]{2,1,0:T(8,128)(2,1)S(1)} %copy-done.4), kind=kOutput, calls=%fused_computation.5 | convolution fusion | flops 3221225472 | bytes 11534336 | tf_op jit(solution)/shard_map/dot_general | solution.py:399
  138.3 2.1 fusion.17.src_ref
  140.4 36.9 %shard_map.92 = bf16[4,1536,256]{2,1,0:T(8,128)(2,1)} custom-call(bf16[1536,256]{1,0:T(8,128)(2,1)} %fusion.17.src_ref), custom_call_target="tpu_custom_call" | custom-call | bytes 6291456 | tf_op jit(solution)/shard_map/pallas_call | solution.py:370
  177.4 1.8 convolution_convert_fusion.3
  179.2 1.7 convolution_convert_fusion.2
  180.9 0.6 convolution_convert_fusion.1
  181.5 0.6 convolution_convert_fusion
  182.1 0.6 convolution_convert_fusion.4
  183.2 0.6 convolution_convert_fusion.6
  183.8 2.9 %select_convert_fusion = bf16[1536,512]{1,0:T(8,128)(2,1)} fusion(bf16[1536,512]{1,0:T(8,128)(2,1)S(1)} %convolution_convert_fusion, bf16[1536,512]{1,0:T(8,128)(2,1)S(1)} %convolution_convert_fusion.1, bf16[1536,512]{1,0:T(8,128)(2,1)S(1)} %convolution_convert_fusion.2, bf16[1536,512]{1,0:T(8,128)(2,1)S(1)} %convolution_convert_fusion.3, ...), kind=kOutput, calls=%fused_computation.6 | convolution fusion | flops 416022528 | bytes 13633536 | tf_op jit(solution)/shard_map/dot_general | solution.py:414
  186.7 46.0 %shard_map.93 = bf16[64,24,512]{2,1,0:T(8,128)(2,1)} custom-call(bf16[64,24,512]{2,1,0:T(8,128)(2,1)} %bitcast.95), custom_call_target="tpu_custom_call" | custom-call | bytes 3145728 | tf_op jit(solution)/shard_map/pallas_call | solution.py:113
  232.7 1.5 concatenate.3
  234.2 4.0 %gather_fusion = bf16[1024,512]{1,0:T(8,128)(2,1)S(1)} fusion(bf16[1537,512]{1,0:T(8,128)(2,1)S(1)} %concatenate.3, s32[1024]{0:T(1024)S(1)} %broadcast_clamp_fusion), kind=kCustom, calls=%fused_computation.1 | custom fusion | bytes 2101248 | tf_op jit(solution)/shard_map/gather | solution.py:495
  238.2 0.7 fusion
  238.8 1.6 add_convert_fusion
  (49 shorter events, 3.6 us)
Async XLA Ops:
  0.0 8.7 %copy-start = (bf16[2048,64]{0,1:T(8,128)(2,1)S(1)}, bf16[2048,64]{0,1:T(8,128)(2,1)}, u32[]{:S(2)}) copy-start(bf16[2048,64]{0,1:T(8,128)(2,1)} %param.11) | copy-start | bytes 786436
  9.0 7.2 %copy-start.6 = (s32[128]{0:T(128)S(1)}, s32[128]{0:T(128)}, u32[]{:S(2)}) copy-start(s32[128]{0:T(128)} %param.14) | copy-start | bytes 1540
  16.4 1.4 copy-start.7
  16.9 1.3 copy-start.5
  42.7 86.5 %copy-start.3 = (bf16[4,512,512]{2,1,0:T(8,128)(2,1)S(1)}, bf16[4,512,512]{2,1,0:T(8,128)(2,1)}, u32[]{:S(2)}) copy-start(bf16[4,512,512]{2,1,0:T(8,128)(2,1)} %reshape_squeeze.7) | copy-start | bytes 6291460
  129.2 5.7 %copy-start.4 = (bf16[4,512,512]{2,1,0:T(8,128)(2,1)S(1)}, bf16[4,512,512]{2,1,0:T(8,128)(2,1)}, u32[]{:S(2)}) copy-start(bf16[4,512,512]{2,1,0:T(8,128)(2,1)} %reshape_squeeze.6) | copy-start | bytes 6291460
  129.2 5.7 %copy-start.8 = (bf16[4,64,24,512]{3,2,1,0:T(8,128)(2,1)S(1)}, bf16[4,64,24,512]{3,2,1,0:T(8,128)(2,1)}, u32[]{:S(2)}) copy-start(bf16[4,64,24,512]{3,2,1,0:T(8,128)(2,1)} %get-tuple-element.7) | copy-start | bytes 18874372
  140.4 36.9 %copy-start.2 = (bf16[4,2,256,512]{3,2,1,0:T(8,128)(2,1)S(1)}, bf16[4,2,256,512]{3,2,1,0:T(8,128)(2,1)}, u32[]{:S(2)}) copy-start(bf16[4,2,256,512]{3,2,1,0:T(8,128)(2,1)} %get-tuple-element.8) | copy-start | bytes 6291460
  177.4 3.6 %copy-start.1 = (bf16[4,1536,256]{2,1,0:T(8,128)(2,1)S(1)}, bf16[4,1536,256]{2,1,0:T(8,128)(2,1)}, u32[]{:S(2)}) copy-start(bf16[4,1536,256]{2,1,0:T(8,128)(2,1)} %shard_map.92) | copy-start | bytes 9437188

commit v7 on v6

--- a/solution.py
+++ b/solution.py
@@ -448,7 +448,9 @@
     scale = lax.rsqrt(jnp.mean(hidden * hidden, axis=-1, keepdims=True) + 1e-06)
     normed = (hidden * scale * norm_gain.astype(jnp.float32)).astype(jnp.bfloat16)
     logits = jnp.dot(normed, routing_projection_matrix, preferred_element_type=jnp.float32)
-    score = jax.nn.sigmoid(jnp.take_along_axis(logits, experts, axis=1)).reshape(-1)
+    expert_ids = jnp.arange(logits.shape[1], dtype=jnp.int32)
+    chosen = jnp.where(experts[:, :, None] == expert_ids[None, None, :], logits[:, None, :], 0.0)
+    score = jax.nn.sigmoid(jnp.sum(chosen, axis=2)).reshape(-1)
 
     slot_ids = assign_slots(experts, replica_key, slot_expert)
     onehot = (slot_ids[:, None] == jnp.arange(slot_count, dtype=jnp.int32)[None, :]).astype(
@@ -462,15 +464,13 @@
     target = jnp.where(
         kept_mask, slot_ids // per_device * buffer_rows + row_in, peer_count * buffer_rows
     )
-    source_rows = jnp.arange(rows_here * pick_count, dtype=jnp.int32) // pick_count
 
     normed_part = lax.dynamic_slice_in_dim(normed, group_pos * quarter, quarter, 1)
-    outgoing = (
-        jnp.zeros((peer_count * buffer_rows + 1, quarter), jnp.bfloat16)
-        .at[target]
-        .set(normed_part[source_rows])
-    )
-    outgoing = outgoing[:-1].reshape(peer_count, buffer_rows, quarter)
+    buffer_ids = jnp.arange(peer_count * buffer_rows, dtype=jnp.int32)
+    hits = target.reshape(rows_here, pick_count)[None, :, :] == buffer_ids[:, None, None]
+    placement = jnp.any(hits, axis=2).astype(jnp.bfloat16)
+    outgoing = jnp.dot(placement, normed_part, preferred_element_type=jnp.float32)
+    outgoing = outgoing.astype(jnp.bfloat16).reshape(peer_count, buffer_rows, quarter)
     full_in, down_parts = dispatch(outgoing, down_weight)
     quarters = full_in.reshape(group_count, peer_count * buffer_rows, quarter)
 

time: 244 us -> 238 us (0.975)
  local copies, waits for them, and re-layouts: 40.9 us -> 21.5 us
  matrix products: 18.6 us -> 28.4 us
  other arithmetic: 11.2 us -> 16.2 us
    scatter x1 -> x0, local copies, waits for them, and re-layouts: 10.3 us -> none  [on_device(): outgoing = jnp.zeros((peer_count * buffer_rows + 1, quarter), jnp.bfloat1...]
    dot_general x2, matrix products: 9.07 us -> 17.2 us  [slot_activated(): lax.dot_general(quarters, gate_up_one.reshape(group_count, quarter, 2 * u...]
    gather x5 -> x0, local copies, waits for them, and re-layouts: 7.34 us -> none  [on_device(): jnp.take_along_axis(logits, experts, axis=1)]
    reduce_or x0 -> x1, other arithmetic: none -> 5.75 us  [on_device(): placement = jnp.any(hits, axis=2).astype(jnp.bfloat16)]
where the time goes in v7:
time: 238 us; the launch traced here: 235 us
  Pallas kernels  169 us (71%)
  matrix products  28.4 us (12%)
  local copies, waits for them, and re-layouts  21.5 us (9%)
  other arithmetic  16.2 us (7%)
    pallas_call x1, Pallas kernels, dispatch(): pl.pallas_call(functools.partial(dispatch_kernel, n_exp, n_dp), out_shape...  86.2 us
    pallas_call x1, Pallas kernels, exchange(): pl.pallas_call(functools.partial(exchange_kernel, n_exp, n_dp, with_down)...  46.1 us
    pallas_call x1, Pallas kernels, gather_dp(): pl.pallas_call(functools.partial(gather_kernel, n_dp), out_shape=jax.Shap...  36.8 us
    dot_general x2, matrix products, slot_activated(): lax.dot_general(quarters, gate_up_one.reshape(group_count, quarter, 2 * u...  17.2 us
    dot_general x8, matrix products, group_sums(): jnp.dot(act_all[group], down_cols[lower:lower + unit_count], preferred_el...  9.22 us
    another operation x2, local copies, waits for them, and re-layouts, slot_activated(): gate_up_one.reshape(group_count, quarter, 2 * unit_count)  7 us
    reduce_or x1, other arithmetic, on_device(): placement = jnp.any(hits, axis=2).astype(jnp.bfloat16)  5.75 us
    slice x1, local copies, waits for them, and re-layouts, on_device(): second_act = slot_activated(quarters, slot_gate_up_weight[1])  5.68 us

profile of v7, /device:TPU:89, one launch (start us, length us, event | category | flops | bytes accessed | tf_op | source)
XLA Modules:
  0.0 235.5 jit_solution(8999532381998685973)
XLA Ops:
  0.0 0.8 copy.19
  0.9 0.8 compare_convert_fusion
  1.7 0.5 reduce_window_sum.26
  2.2 0.8 convert_reduce_fusion
  3.0 0.8 copy.20
  4.0 0.9 fusion.26
  6.5 0.3 fusion.46
  7.1 5.7 %fusion = pred[1536,128]{1,0:T(8,128)(4,1)S(1)} fusion(s32[128,8]{0,1:T(8,128)S(1)} %fusion.40), kind=kLoop, calls=%fused_computation.2 | loop fusion | flops 2949120 | bytes 200704 | tf_op jit(solution)/shard_map/reduce_or | solution.py:471
  12.9 1.7 convolution_convert_fusion.8
  14.6 86.2 %shard_map.91 = (bf16[4,64,24,512]{3,2,1,0:T(8,128)(2,1)}, bf16[4,2,256,512]{3,2,1,0:T(8,128)(2,1)}) custom-call(bf16[64,24,512]{2,1,0:T(8,128)(2,1)} %bitcast.88, bf16[2,256,2048]{2,1,0:T(8,128)(2,1)} %down_ref.1), custom_call_target="tpu_custom_call" | custom-call | bytes 16777216 | tf_op jit(solution)/shard_map/pallas_call | solution.py:312
  100.7 5.7 %fusion.45 = (bf16[1,2048,2,256]{3,2,1,0:T(2,128)(2,1)}, bf16[1,2048,2,256]{3,2,1,0:T(2,128)(2,1)S(1)}) fusion(bf16[2,2048,2,256]{3,2,1,0:T(2,128)(2,1)} %param.16), kind=kLoop, calls=%fused_computation.107 | loop fusion | bytes 8388608 | tf_op jit(solution)/shard_map/slice | solution.py:478
  106.4 4.4 %reshape_squeeze.7 = bf16[4,512,512]{2,1,0:T(8,128)(2,1)} reshape(bf16[1,2048,2,256]{3,2,1,0:T(2,128)(2,1)} %get-tuple-element.13) | data formatting | bytes 4194304 | tf_op jit(solution)/shard_map/reshape;squeeze | solution.py:401
  110.8 8.5 %convolution_bitcast_fusion = f32[1536,512]{1,0:T(8,128)} fusion(bf16[4,1536,512]{2,1,0:T(8,128)(2,1)} %bitcast.105, bf16[4,512,512]{2,1,0:T(8,128)(2,1)} %reshape_squeeze.7), kind=kOutput, calls=%fused_computation.3 | convolution fusion | flops 3221225472 | bytes 11534336 | tf_op jit(solution)/shard_map/dot_general | solution.py:399
  119.4 2.6 %reshape_squeeze.6 = bf16[4,512,512]{2,1,0:T(8,128)(2,1)} reshape(bf16[1,2048,2,256]{3,2,1,0:T(2,128)(2,1)S(1)} %get-tuple-element.14) | data formatting | bytes 4194304 | tf_op jit(solution)/shard_map/reshape;squeeze | solution.py:401
  122.0 8.6 %convolution_bitcast_fusion.1 = f32[1536,512]{1,0:T(8,128)} fusion(bf16[4,1536,512]{2,1,0:T(8,128)(2,1)} %bitcast.106, bf16[4,512,512]{2,1,0:T(8,128)(2,1)} %reshape_squeeze.6), kind=kOutput, calls=%fused_computation.4 | convolution fusion | flops 3221225472 | bytes 11534336 | tf_op jit(solution)/shard_map/dot_general | solution.py:399
  130.6 0.6 dynamic_slice.11
  131.2 0.7 fusion.34
  131.8 3.4 %fusion.15.src_ref = bf16[1536,256]{1,0:T(8,128)(2,1)} fusion(f32[1536,512]{1,0:T(8,128)} %convolution_bitcast_fusion.1, f32[1536,512]{1,0:T(8,128)S(1)} %copy-done.2, pred[1536]{0:T(1024)(128)(4,1)S(1)} %fusion.34), kind=kLoop, calls=%fused_computation.34 | loop fusion | flops 5111808 | bytes 7079424 | tf_op jit(solution)/shard_map/jit(_where)/select_n | solution.py:482
  135.3 36.8 %shard_map.92 = bf16[4,1536,256]{2,1,0:T(8,128)(2,1)} custom-call(bf16[1536,256]{1,0:T(8,128)(2,1)} %fusion.15.src_ref), custom_call_target="tpu_custom_call" | custom-call | bytes 6291456 | tf_op jit(solution)/shard_map/pallas_call | solution.py:370
  172.1 1.9 convolution_convert_fusion.6
  174.0 1.7 convolution_convert_fusion.5
  175.7 0.6 convolution_convert_fusion.4
  176.2 0.6 convolution_convert_fusion.3
  176.8 0.6 convolution_convert_fusion.2
  177.4 0.6 convolution_convert_fusion.1
  178.0 0.6 convolution_convert_fusion
  178.5 2.8 %select_convert_fusion = bf16[1536,512]{1,0:T(8,128)(2,1)} fusion(bf16[1536,512]{1,0:T(8,128)(2,1)S(1)} %convolution_convert_fusion, bf16[1536,512]{1,0:T(8,128)(2,1)S(1)} %convolution_convert_fusion.1, bf16[1536,512]{1,0:T(8,128)(2,1)S(1)} %convolution_convert_fusion.2, bf16[1536,512]{1,0:T(8,128)(2,1)S(1)} %convolution_convert_fusion.3, ...), kind=kOutput, calls=%fused_computation.5 | convolution fusion | flops 416022528 | bytes 13633536 | tf_op jit(solution)/shard_map/dot_general | solution.py:414
  181.4 46.1 %shard_map.93 = bf16[64,24,512]{2,1,0:T(8,128)(2,1)} custom-call(bf16[64,24,512]{2,1,0:T(8,128)(2,1)} %bitcast.90), custom_call_target="tpu_custom_call" | custom-call | bytes 3145728 | tf_op jit(solution)/shard_map/pallas_call | solution.py:113
  227.5 1.5 concatenate.3
  229.1 4.0 %gather_fusion = bf16[1024,512]{1,0:T(8,128)(2,1)S(1)} fusion(bf16[1537,512]{1,0:T(8,128)(2,1)S(1)} %concatenate.3, s32[1024]{0:T(1024)S(1)} %broadcast_clamp_fusion), kind=kCustom, calls=%fused_computation | custom fusion | bytes 2101248 | tf_op jit(solution)/shard_map/gather | solution.py:495
  233.2 0.7 fusion.1
  233.9 1.6 add_convert_fusion
  (43 shorter events, 2.2 us)
Async XLA Ops:
  0.0 6.5 %copy-start = (bf16[2048,64]{0,1:T(8,128)(2,1)S(1)}, bf16[2048,64]{0,1:T(8,128)(2,1)}, u32[]{:S(2)}) copy-start(bf16[2048,64]{0,1:T(8,128)(2,1)} %param.11) | copy-start | bytes 786436
  1.7 3.9 %copy-start.7 = (s32[128]{0:T(128)S(1)}, s32[128]{0:T(128)}, u32[]{:S(2)}) copy-start(s32[128]{0:T(128)} %param.15) | copy-start | bytes 1540
  3.9 2.2 copy-start.6
  3.9 2.2 copy-start.3
  5.3 1.5 copy-start.5
  122.0 9.9 %copy-start.2 = (f32[1536,512]{1,0:T(8,128)S(1)}, f32[1536,512]{1,0:T(8,128)}, u32[]{:S(2)}) copy-start(f32[1536,512]{1,0:T(8,128)} %convolution_bitcast_fusion) | copy-start | bytes 9437188
  135.3 36.8 %copy-start.4 = (bf16[4,2,256,512]{3,2,1,0:T(8,128)(2,1)S(1)}, bf16[4,2,256,512]{3,2,1,0:T(8,128)(2,1)}, u32[]{:S(2)}) copy-start(bf16[4,2,256,512]{3,2,1,0:T(8,128)(2,1)} %get-tuple-element.8) | copy-start | bytes 6291460
  172.1 3.6 %copy-start.1 = (bf16[4,1536,256]{2,1,0:T(8,128)(2,1)S(1)}, bf16[4,1536,256]{2,1,0:T(8,128)(2,1)}, u32[]{:S(2)}) copy-start(bf16[4,1536,256]{2,1,0:T(8,128)(2,1)} %shard_map.92) | copy-start | bytes 9437188
